TPU v7x, 256 devices: a whole 4x4x8 slice. The times are simulated.
256 devices in a mesh: req: 64 (over x, y, z_hi), tp: 4 (over z_lo, core).
Axes of the slice: x: 4, y: 4, z: 8 (z_hi: 4, z_lo: 2; z = z_hi * 2 + z_lo), core: 2. Of those that a mesh axis runs over, the one named last changes fastest.
Arguments:
- hidden: bfloat16 [64, 256, 4, 2432], P('req'), may hold values from -4 to 4
- modulation: bfloat16 [16, 4, 3, 2432], replicated, may hold values from -4 to 4
- w_qkv: bfloat16 [2432, 3, 1536], P(None, None, 'tp'), may hold values from -0.125 to 0.125
- w_out: bfloat16 [1536, 2432], P('tp'), may hold values from -0.75 to 0.75
- qk_gain: float32 [2, 64], replicated, may hold values from 0.1 to 1.9
- stale_kv: bfloat16 [64, 256, 4, 2, 1536], P('req', None, None, None, 'tp'), may hold values from -5 to 5
- text_kv: bfloat16 [64, 40, 4, 2, 1536], P('req', None, None, None, 'tp'), may hold values from -5 to 5
- text_len: int32 [16, 4], replicated, may hold values from 1 to 160, as said below
Outputs:
- updated: bfloat16 [64, 256, 4, 2432], P('req', 'tp')
- fresh_kv: bfloat16 [64, 256, 4, 2, 1536], P('req', None, None, None, 'tp')
Inputs may be any that keep to these rules, and one draw needn't show every extreme that they name: `text_len`: some item has all 160 text tokens valid in every draw.
All inputs are finite; a program needn't handle non-finite values.
Results may differ from a plain program's by a relative error of at most 0.015.
Values may be sent and summed in bfloat16 or wider, within the bound.
No kernel may reach another device: no remote copies, remote signals or barrier semaphores. Data moves between devices by JAX's collectives and lax.ppermute only.
A program may use at most 128 MiB of HBM per device.

v0:
```python
import jax
import jax.numpy as jnp
from jax import lax
from jax.sharding import PartitionSpec as P

HEAD = 64
PATCHES = 4


EPSILON = 1e-06


def from_behind(value, axis, by):
    length = lax.axis_size(axis)
    return lax.ppermute(value, axis, [(i, (i + by) % length) for i in range(length)])


def modulate(rows_in, mod_rows):
    values_f = rows_in.astype(jnp.float32)
    center = values_f - jnp.mean(values_f, axis=-1, keepdims=True)
    variance = jnp.mean(center * center, axis=-1, keepdims=True)
    normed = center * lax.rsqrt(variance + EPSILON)
    shift_rows = mod_rows[:, 0, :].astype(jnp.float32)
    scale_rows = mod_rows[:, 1, :].astype(jnp.float32)
    return (normed * (1.0 + scale_rows) + shift_rows).astype(jnp.bfloat16)


def head_norm(heads_in, gain_row):
    square = jnp.mean(heads_in * heads_in, axis=-1, keepdims=True)
    return (heads_in * lax.rsqrt(square + EPSILON) * gain_row).astype(jnp.bfloat16)


def attend(query_heads, key_heads, value_heads, valid):
    scores = (
        jnp.einsum("rbhe,kbhe->bhrk", query_heads, key_heads, preferred_element_type=jnp.float32)
        * 0.125
    )
    weights = jnp.exp(scores) * jnp.transpose(valid)[:, None, None, :]
    probs = (weights / jnp.sum(weights, axis=-1, keepdims=True)).astype(jnp.bfloat16)
    return jnp.einsum(
        "bhrk,kbhe->rbhe", probs, value_heads, preferred_element_type=jnp.float32
    ).astype(jnp.bfloat16)


def body(hidden, modulation, w_qkv, w_out, qk_gain, stale_kv, text_kv, text_len):
    slots = lax.axis_size("req")
    groups = slots // PATCHES
    place = lax.axis_index("req")
    group = place % groups
    patch = place // groups
    rows_in = hidden[0]
    row_total, items, width_d = rows_in.shape
    local_width = w_out.shape[0]
    local_heads = local_width // HEAD
    text_rows = text_kv.shape[1]
    mod_rows = lax.dynamic_index_in_dim(modulation, group, 0, keepdims=False)
    lengths = lax.dynamic_index_in_dim(text_len, group, 0, keepdims=False)
    offsets = [groups, 2 * groups, 3 * groups]
    received = []
    for offset in offsets:
        arrived = from_behind((stale_kv[0], text_kv[0]), "req", offset)
        received.append((offset // groups, arrived))
    modulated = modulate(rows_in, mod_rows)
    projections = jnp.dot(
        modulated.reshape(-1, width_d),
        w_qkv.reshape(width_d, -1),
        preferred_element_type=jnp.float32,
    )
    projections = projections.reshape(row_total, items, 3, local_heads, HEAD)
    query_heads = head_norm(projections[:, :, 0], qk_gain[0])
    key_heads = head_norm(projections[:, :, 1], qk_gain[1])
    value_heads = projections[:, :, 2].astype(jnp.bfloat16)
    fresh_pairs = jnp.stack(
        [
            key_heads.reshape(row_total, items, local_width),
            value_heads.reshape(row_total, items, local_width),
        ],
        axis=2,
    )
    image_parts = [fresh_pairs] + [entry[1][0] for entry in received]
    text_parts = [text_kv[0]] + [entry[1][1] for entry in received]
    owners = [patch] + [jnp.mod(patch - entry[0], PATCHES) for entry in received]
    position = jnp.arange(text_rows, dtype=jnp.int32)
    text_masks = [
        ((owner * text_rows + position)[:, None] < lengths[None, :]).astype(jnp.float32)
        for owner in owners
    ]
    all_pairs = jnp.concatenate(image_parts + text_parts, axis=0)
    valid = jnp.concatenate(
        [jnp.ones((len(image_parts) * row_total, items), jnp.float32)] + text_masks, axis=0
    )
    all_keys = all_pairs[:, :, 0].reshape(-1, items, local_heads, HEAD)
    all_values = all_pairs[:, :, 1].reshape(-1, items, local_heads, HEAD)
    mixed = attend(query_heads, all_keys, all_values, valid).reshape(row_total, items, local_width)
    share = row_total // lax.axis_size("tp")
    summed = lax.psum_scatter(
        jnp.einsum("rbe,ed->rbd", mixed, w_out, preferred_element_type=jnp.float32).astype(
            jnp.bfloat16
        ),
        "tp",
        scatter_dimension=0,
        tiled=True,
    ).astype(jnp.float32)
    own_rows = lax.dynamic_slice_in_dim(rows_in, lax.axis_index("tp") * share, share, 0)
    gate_rows = mod_rows[:, 2, :].astype(jnp.float32)
    updated = (own_rows.astype(jnp.float32) + gate_rows[None] * summed).astype(jnp.bfloat16)
    return (updated[None], fresh_pairs[None])


def solution(mesh):
    return jax.shard_map(
        body,
        mesh=mesh,
        in_specs=(
            P("req", None, None, None),
            P(),
            P(None, None, "tp"),
            P("tp", None),
            P(),
            P("req", None, None, None, "tp"),
            P("req", None, None, None, "tp"),
            P(),
        ),
        out_specs=(P("req", "tp", None, None), P("req", None, None, None, "tp")),
        check_vma=False,
    )
```

profile of v0, /device:TPU:1, one launch (start us, length us, event | category | flops | bytes accessed | tf_op | source)
XLA Modules:
  0.0 216.7 jit_solution(15149891152339655918)
XLA Ops:
  7.2 5.0 %copy.30 = bf16[1,256,4,2,384]{1,4,2,3,0:T(8,128)(2,1)} copy(bf16[1,256,4,2,384]{4,3,2,1,0:T(2,128)(2,1)} %param.13) | data formatting | bytes 3145728 | tf_op args[5]
  12.3 2.0 collective-permute-start
  14.3 2.5 %collective-permute-start.1 = (bf16[256,4,2,384]{0,3,1,2:T(8,128)(2,1)}, bf16[256,4,2,384]{0,3,1,2:T(8,128)(2,1)}, u32[]{:S(2)}, u32[]{:S(2)}) collective-permute-start(bf16[256,4,2,384]{0,3,1,2:T(8,128)(2,1)} %bitcast.16), channel_id=1, source_target_pairs={{0,128},{4,132},{8,136},{12,140},{16,144},{20,148},{24,152},{28,15... | collective-permute-start | bytes 4718600 | tf_op jit(solution)/shard_map/ppermute | solution.py:15
  16.8 1.2 collective-permute-start.2
  17.9 1.7 copy.55
  19.9 0.9 collective-permute-start.4
  20.8 0.8 dynamic-slice_bitcast_fusion
  22.9 8.7 %copy.28 = bf16[2432,3,384]{0,2,1:T(8,128)(2,1)} copy(bf16[2432,3,384]{2,0,1:T(8,128)(2,1)} %param.10) | data formatting | bytes 11206656 | tf_op args[2]
  31.6 4.4 %convert_reduce_fusion = f32[256,4]{1,0:T(8,128)S(1)} fusion(bf16[1,256,4,2432]{3,2,1,0:T(4,128)(2,1)} %param.8), kind=kLoop, calls=%fused_computation.5 | loop fusion | flops 4979712 | bytes 4984832 | tf_op jit(solution)/shard_map/reduce_sum | solution.py:20
  36.0 5.8 %fusion.8 = f32[256,4]{1,0:T(8,128)S(1)} fusion(bf16[1,256,4,2432]{3,2,1,0:T(4,128)(2,1)} %param.8, f32[256,4]{1,0:T(8,128)S(1)} %broadcast_multiply_fusion), kind=kLoop, calls=%fused_computation.13 | loop fusion | flops 9960448 | bytes 4988928 | tf_op jit(solution)/shard_map/reduce_sum | solution.py:21
  41.9 6.6 %fusion.9 = bf16[256,4,2432,1,1]{2,1,0,4,3:T(4,128)(2,1)S(1)} fusion(bf16[1,256,4,2432]{3,2,1,0:T(4,128)(2,1)} %param.8, f32[4,2432]{1,0:T(4,128)} %get-tuple-element.15, f32[4,2432]{1,0:T(4,128)} %add_bitcast_fusion, f32[256,4]{1,0:T(8,128)S(1)} %add_rsqrt_fusion, f32[256,4]{1,0:T(8,128)S(1)} %broadcast_multiply_fusion), kind=kLoop, calls=%fused_computation.15 | loop fusion | flops 14942208 | bytes 10047488 | tf_op jit(solution)/shard_map/convert_element_type | solution.py:25
  48.5 6.4 %fusion.10 = f32[256,4,3,6,64]{0,4,3,2,1:T(8,128)S(1)} fusion(bf16[3,6,64,2432,1]{3,2,1,0,4:T(8,128)(2,1)S(1)} %bitcast.87, bf16[256,4,2432,1,1]{2,1,0,4,3:T(4,128)(2,1)S(1)} %fusion.9), kind=kOutput, calls=%fused_computation.16 | convolution fusion | flops 5737807872 | bytes 15302656 | tf_op jit(solution)/shard_map/dot_general | solution.py:64
  55.4 1.6 copy-done.1
  57.0 1.0 slice.66
  58.6 27.9 %collective-permute-done.3 = bf16[40,4,2,384]{3,0,2,1:T(8,128)(2,1)} collective-permute-done((bf16[40,4,2,384]{3,0,2,1:T(8,128)(2,1)}, bf16[40,4,2,384]{3,0,2,1:T(8,128)(2,1)}, u32[]{:S(2)}, u32[]{:S(2)}) %collective-permute-start.3) | collective-permute-done | bytes 245792 | tf_op jit(solution)/shard_map/ppermute | solution.py:15
  86.4 3.7 %collective-permute-start.5 = (bf16[40,4,2,384]{3,0,2,1:T(8,128)(2,1)}, bf16[40,4,2,384]{3,0,2,1:T(8,128)(2,1)}, u32[]{:S(2)}, u32[]{:S(2)}) collective-permute-start(bf16[40,4,2,384]{3,0,2,1:T(8,128)(2,1)} %bitcast.82), channel_id=1, source_target_pairs={{0,192},{4,196},{8,200},{12,204},{16,208},{20,212},{24,216},{28,22... | collective-permute-start | bytes 737288 | tf_op jit(solution)/shard_map/ppermute | solution.py:15
  90.2 2.5 %fusion.24 = (bf16[1,256,4,2,384]{1,4,2,3,0:T(8,128)(2,1)}, bf16[256,4,2,384]{0,3,1,2:T(8,128)(2,1)S(1)}) fusion(bf16[256,4,1,384]{0,3,1,2:T(8,128)(2,1)} %bitcast.90, bf16[256,4,1,384]{0,3,1,2:T(8,128)(2,1)S(1)} %fusion.15), kind=kLoop, calls=%fused_computation.60 | loop fusion | flops 786432 | bytes 4718592 | tf_op jit(solution)/shard_map/broadcast_in_dim | solution.py:107
  92.7 2.1 copy.31
  94.8 2.2 copy.35
  97.0 2.1 copy.36
  99.1 2.1 copy.37
  101.2 12.6 %concatenate.6 = bf16[1184,4,2,384]{0,3,1,2:T(8,128)(2,1)} concatenate(bf16[256,4,2,384]{0,3,1,2:T(8,128)(2,1)S(1)} %get-tuple-element.13, bf16[256,4,2,384]{0,3,1,2:T(8,128)(2,1)} %collective-permute-done, bf16[256,4,2,384]{0,3,1,2:T(8,128)(2,1)} %collective-permute-done.1, bf16[256,4,2,384]{0,3,1,2:T(8,128)(2,1)} %collective-permute-done.2, bf16[40,4,2,384]{0,3,1,2:T(8,128)(2,1)} %bitcast.89, ...), dimensions={0} | concatenate | bytes 14548992 | tf_op jit(solution)/shard_map/concatenate | solution.py:88
  113.8 3.6 %fusion.25 = (bf16[1184,4,1,384]{0,3,1,2:T(8,128)(2,1)S(1)}, bf16[1184,4,1,384]{0,3,1,2:T(8,128)(2,1)S(1)}) fusion(bf16[1184,4,2,384]{0,3,1,2:T(8,128)(2,1)} %concatenate.6), kind=kLoop, calls=%fused_computation.61 | loop fusion | bytes 14548992 | tf_op jit(solution)/shard_map/slice | solution.py:92
  117.4 14.0 %fusion = (f32[4,6,256]{2,1,0:T(8,128)S(1)}, f32[4,6,256,1184]{2,3,1,0:T(8,128)}) fusion(f32[4,1184]{1,0:T(4,128)S(1)} %bitcast.91, bf16[1184,4,6,64]{0,3,2,1:T(8,128)(2,1)S(1)} %bitcast.83, f32[256,4,3,6,64]{0,4,3,2,1:T(8,128)} %copy-done.1, f32[64]{0:T(128)S(1)} %get-tuple-element.16, f32[256,4,6]{0,2,1:T(8,128)S(1)} %add_rsqrt_fusion.1), kind=kOutput, calls=%fused_computation.2 | convolution fusion | flops 954132480 | bytes 34376448 | tf_op jit(solution)/shard_map/rbhe,kbhe->bhrk/dot_general | solution.py:35
  131.4 12.4 %fusion.16 = bf16[4,6,64,256]{3,2,1,0:T(8,128)(2,1)S(1)} fusion(bf16[1184,4,6,64]{0,3,2,1:T(8,128)(2,1)S(1)} %bitcast.88, f32[4,6,256,1184]{2,3,1,0:T(8,128)} %get-tuple-element.23, f32[4,6,256]{2,1,0:T(8,128)S(1)} %get-tuple-element.22, f32[4,1184]{1,0:T(4,128)S(1)} %bitcast.92), kind=kOutput, calls=%fused_computation.30 | convolution fusion | flops 960626688 | bytes 33565184 | tf_op jit(solution)/shard_map/bhrk,kbhe->rbhe/dot_general | solution.py:40
  143.8 4.6 %convolution_convert_fusion = bf16[256,4,2432]{2,0,1:T(8,128)(2,1)} fusion(bf16[256,4,384]{0,2,1:T(8,128)(2,1)S(1)} %bitcast.93, bf16[384,2432]{1,0:T(8,128)(2,1)S(1)} %copy-done), kind=kOutput, calls=%fused_computation.14 | convolution fusion | flops 1915092992 | bytes 7634944 | tf_op jit(solution)/shard_map/rbe,ed->rbd/dot_general | solution.py:97
  148.4 1.4 copy-done.2
  149.8 3.0 %copy.40 = bf16[1,256,4,2,384]{4,3,2,1,0:T(2,128)(2,1)} copy(bf16[1,256,4,2,384]{1,4,2,3,0:T(8,128)(2,1)S(1)} %copy-done.2) | data formatting | bytes 3145728
  152.8 1.7 constant_dynamic-slice_fusion
  154.6 51.7 %reduce-scatter.2.cloned.1.call-done = bf16[64,4,2432]{2,0,1:T(8,128)(2,1)} async-done(((bf16[256,4,2432]{2,0,1:T(8,128)(2,1)}), bf16[64,4,2432]{2,0,1:T(8,128)(2,1)}) %reduce-scatter.2.cloned.1.call-update) | async-done | bytes 1245200 | tf_op jit(solution)/shard_map/reduce_scatter | solution.py:96
  206.3 1.6 fusion.17
  207.9 2.0 copy.39
  (41 shorter events, 2.9 us)
Async XLA Ops:
  7.2 136.7 %copy-start = (bf16[384,2432]{1,0:T(8,128)(2,1)S(1)}, bf16[384,2432]{1,0:T(8,128)(2,1)}, u32[]{:S(2)}) copy-start(bf16[384,2432]{1,0:T(8,128)(2,1)} %param.11) | copy-start | bytes 5603332
  7.2 199.1 %reduce-scatter.2.cloned.1.call-start = ((), (), s32[]{:S(2)}) async-start(), calls=%async_computation.1 | async-start | bytes 6225920 | tf_op jit(solution)/shard_map/reduce_scatter | solution.py:96
  12.3 89.0 %collective-permute-start = (bf16[256,4,2,384]{0,3,1,2:T(8,128)(2,1)}, bf16[256,4,2,384]{0,3,1,2:T(8,128)(2,1)}, u32[]{:S(2)}, u32[]{:S(2)}) collective-permute-start(bf16[256,4,2,384]{0,3,1,2:T(8,128)(2,1)} %bitcast.16), channel_id=1, source_target_pairs={{0,64},{4,68},{8,72},{12,76},{16,80},{20,84},{24,88},{28,92},{32,9... | collective-permute-start | bytes 4718600 | tf_op jit(solution)/shard_map/ppermute | solution.py:15
  14.3 86.9 %collective-permute-start.1 = (bf16[256,4,2,384]{0,3,1,2:T(8,128)(2,1)}, bf16[256,4,2,384]{0,3,1,2:T(8,128)(2,1)}, u32[]{:S(2)}, u32[]{:S(2)}) collective-permute-start(bf16[256,4,2,384]{0,3,1,2:T(8,128)(2,1)} %bitcast.16), channel_id=1, source_target_pairs={{0,128},{4,132},{8,136},{12,140},{16,144},{20,148},{24,152},{28,15... | collective-permute-start | bytes 4718600 | tf_op jit(solution)/shard_map/ppermute | solution.py:15
  16.8 84.5 %collective-permute-start.2 = (bf16[256,4,2,384]{0,3,1,2:T(8,128)(2,1)}, bf16[256,4,2,384]{0,3,1,2:T(8,128)(2,1)}, u32[]{:S(2)}, u32[]{:S(2)}) collective-permute-start(bf16[256,4,2,384]{0,3,1,2:T(8,128)(2,1)} %bitcast.16), channel_id=1, source_target_pairs={{0,192},{4,196},{8,200},{12,204},{16,208},{20,212},{24,216},{28,22... | collective-permute-start | bytes 4718600 | tf_op jit(solution)/shard_map/ppermute | solution.py:15
  19.6 66.8 %collective-permute-start.3 = (bf16[40,4,2,384]{3,0,2,1:T(8,128)(2,1)}, bf16[40,4,2,384]{3,0,2,1:T(8,128)(2,1)}, u32[]{:S(2)}, u32[]{:S(2)}) collective-permute-start(bf16[40,4,2,384]{3,0,2,1:T(8,128)(2,1)} %bitcast.82), channel_id=1, source_target_pairs={{0,64},{4,68},{8,72},{12,76},{16,80},{20,84},{24,88},{28,92},{32,9... | collective-permute-start | bytes 737288 | tf_op jit(solution)/shard_map/ppermute | solution.py:15
  19.9 77.1 %collective-permute-start.4 = (bf16[40,4,2,384]{3,0,2,1:T(8,128)(2,1)}, bf16[40,4,2,384]{3,0,2,1:T(8,128)(2,1)}, u32[]{:S(2)}, u32[]{:S(2)}) collective-permute-start(bf16[40,4,2,384]{3,0,2,1:T(8,128)(2,1)} %bitcast.82), channel_id=1, source_target_pairs={{0,128},{4,132},{8,136},{12,140},{16,144},{20,148},{24,152},{28,15... | collective-permute-start | bytes 737288 | tf_op jit(solution)/shard_map/ppermute | solution.py:15
  41.8 6.7 %slice-start = ((s8[5603328]{0:T(1024)(128)(4,1)}), s8[1409024]{0:T(1024)(128)(4,1)S(1)}, s32[]{:S(2)}) async-start(s8[5603328]{0:T(1024)(128)(4,1)} %bitcast.85), calls=%async_computation.2 | async-start | bytes 2818048
  41.9 6.6 %slice-start.1 = ((s8[5603328]{0:T(1024)(128)(4,1)}), s8[4194304]{0:T(1024)(128)(4,1)S(1)}, s32[]{:S(2)}) async-start(s8[5603328]{0:T(1024)(128)(4,1)} %bitcast.85), calls=%async_computation.3 | async-start | bytes 8388608
  48.5 6.6 %copy-start.5 = (f32[2,64]{1,0:T(2,128)S(1)}, f32[2,64]{1,0:T(2,128)}, u32[]{:S(2)}) copy-start(f32[2,64]{1,0:T(2,128)} %param.12) | copy-start | bytes 1540
  54.9 2.1 copy-start.1
  54.9 3.2 %copy-start.4 = (s32[16,4]{0,1:T(4,128)S(1)}, s32[16,4]{0,1:T(4,128)}, u32[]{:S(2)}) copy-start(s32[16,4]{0,1:T(4,128)} %param.15) | copy-start | bytes 772
  86.4 12.7 %collective-permute-start.5 = (bf16[40,4,2,384]{3,0,2,1:T(8,128)(2,1)}, bf16[40,4,2,384]{3,0,2,1:T(8,128)(2,1)}, u32[]{:S(2)}, u32[]{:S(2)}) collective-permute-start(bf16[40,4,2,384]{3,0,2,1:T(8,128)(2,1)} %bitcast.82), channel_id=1, source_target_pairs={{0,192},{4,196},{8,200},{12,204},{16,208},{20,212},{24,216},{28,22... | collective-permute-start | bytes 737288 | tf_op jit(solution)/shard_map/ppermute | solution.py:15
  148.4 1.4 copy-start.2
  148.4 57.9 %copy-start.3 = (f32[4,2432]{1,0:T(4,128)S(1)}, f32[4,2432]{1,0:T(4,128)}, u32[]{:S(2)}) copy-start(f32[4,2432]{1,0:T(4,128)} %get-tuple-element.14) | copy-start | bytes 116740
Sparse Core Ops, SparseCore 0:
  148.6 57.6 reduce-scatter.1
where the time goes:
time: 218 us; the launch traced here: 217 us
  waiting for transfers between devices  79.6 us (37%)
  local copies, waits for them, and re-layouts  51.9 us (24%)
  matrix products  37.4 us (17%)
  other arithmetic  23 us (11%)
  between operations  14.3 us (7%)
  starting transfers between devices  10.6 us (5%)
    reduce_scatter x1, waiting for transfers between devices, body(): lax.psum_scatter(jnp.einsum('rbe,ed->rbd', mixed, w_out, preferred_elemen...  51.7 us
    ppermute x6, waiting for transfers between devices, from_behind(): lax.ppermute(value, axis, [(i, (i + by) % length) for i in range(length)])  27.9 us
    unnamed x21, local copies, waits for them, and re-layouts  23.8 us
    dot_general x1, matrix products, attend(): jnp.einsum('rbhe,kbhe->bhrk', query_heads, key_heads, preferred_element_t...  14 us
    concatenate x1, local copies, waits for them, and re-layouts, body(): all_pairs = jnp.concatenate(image_parts + text_parts, axis=0)  12.6 us
    dot_general x1, matrix products, attend(): jnp.einsum('bhrk,kbhe->rbhe', probs, value_heads, preferred_element_type=...  12.4 us
    ppermute x6, starting transfers between devices, from_behind(): lax.ppermute(value, axis, [(i, (i + by) % length) for i in range(length)])  10.6 us
    convert_element_type x1, other arithmetic, modulate(): return (normed * (1.0 + scale_rows) + shift_rows).astype(jnp.bfloat16)  6.59 us
  transfers between devices with their start and end apart: 7, of which 2 were waited for; matrix products, arithmetic and copies ran while one was open for 25% of the time, Pallas kernels for 0%

commit v1 on v0

v1 whole, which is shorter than its diff:
```python
import functools

import jax
import jax.numpy as jnp
from jax import lax
from jax.experimental import pallas as pl
from jax.experimental.pallas import tpu as pltpu
from jax.sharding import PartitionSpec as P

HEAD = 64
PATCHES = 4
EPSILON = 1e-06
LANES = 128
BF = jnp.bfloat16
F32 = jnp.float32
NT = (((1,), (1,)), ((), ()))
COST = pl.CostEstimate(flops=1000, bytes_accessed=1000, transcendentals=0)


def dot(a, b):
    return jnp.dot(a, b, preferred_element_type=F32)


def params(limit_mb, **kw):
    return pltpu.CompilerParams(vmem_limit_bytes=limit_mb << 20, **kw)


def split_bf(value):
    high = value.astype(BF)
    return high, (value - high.astype(F32)).astype(BF)


def block_ones(rows):
    a = lax.broadcasted_iota(jnp.int32, (rows, LANES), 0) % LANES // HEAD
    b = lax.broadcasted_iota(jnp.int32, (rows, LANES), 1) // HEAD
    return (a == b).astype(F32).astype(BF)


def pack_kernel(item_ref, stale_ref, text_ref, out_ref):
    rows = stale_ref.shape[0]
    for j in range(2):
        out_ref[j, 0:rows] = stale_ref[:, j, :]
        out_ref[j, rows:] = text_ref[:, j, :]


def pack(item, stale, text):
    rows, _, _, width = stale.shape
    trows = text.shape[0]
    grid_spec = pltpu.PrefetchScalarGridSpec(
        num_scalar_prefetch=1,
        grid=(1,),
        in_specs=[
            pl.BlockSpec((rows, None, 2, width), lambda s, it: (0, it[0], 0, 0)),
            pl.BlockSpec((trows, None, 2, width), lambda s, it: (0, it[0], 0, 0)),
        ],
        out_specs=pl.BlockSpec((2, rows + trows, width), lambda s, it: (0, 0, 0)),
    )
    return pl.pallas_call(
        pack_kernel,
        grid_spec=grid_spec,
        out_shape=jax.ShapeDtypeStruct((2, rows + trows, width), BF),
        compiler_params=params(58),
        cost_estimate=COST,
        name="pack",
    )(item, stale, text)


def project_kernel(s_ref, hidden_hbm, mod_ref, gain_ref, w_hbm, q_ref, k_ref, v_ref, *scratch):
    w_ref, h_ref, xa_ref, xb_ref, scale_ref, shift_ref, y_ref, sems = scratch
    outs = (q_ref, k_ref, v_ref)
    blocks, rows, items, width_d = h_ref.shape
    width = w_hbm.shape[2]
    tiles = width // LANES
    loads = [
        pltpu.make_async_copy(hidden_hbm.at[pl.ds(b * rows, rows)], h_ref.at[b], sems.at[b]) for b in range(blocks)
    ]
    weights = [
        pltpu.make_async_copy(w_hbm.at[j], w_ref.at[:, pl.ds(j * width, width)], sems.at[blocks + j]) for j in range(3)
    ]
    loads[0].start()
    for copy in weights:
        copy.start()
    for copy in loads[1:]:
        copy.start()
    shift = mod_ref[0].astype(F32)
    scale = 1.0 + mod_ref[1].astype(F32)
    shift_ref[...] = jnp.concatenate([shift, shift], axis=0)
    scale_ref[...] = jnp.concatenate([scale, scale], axis=0)
    wide = 2 * LANES
    r = lax.broadcasted_iota(jnp.int32, (2 * wide, wide), 0) % wide // HEAD
    c = lax.broadcasted_iota(jnp.int32, (2 * wide, wide), 1) // HEAD
    ones = (r == c).astype(F32).astype(BF)

    def norm_rows(block, x_ref, c):
        x = h_ref[block, c * 4 : c * 4 + 4].reshape(16, width_d).astype(F32).reshape(2, 8, width_d)
        center = x - jnp.mean(x, axis=-1, keepdims=True)
        variance = jnp.mean(center * center, axis=-1, keepdims=True)
        normed = center * lax.rsqrt(variance + EPSILON)
        out = normed * scale_ref[...][None] + shift_ref[...][None]
        x_ref[c * 16 : c * 16 + 16, :] = out.reshape(16, width_d).astype(BF)

    def finish_tile(block, n, y):
        if n + wide <= 2 * width:
            high, low = split_bf(y * y)
            square = dot(jnp.concatenate([high, low], axis=1), ones) * (1.0 / HEAD)
            y = y * lax.rsqrt(square + EPSILON) * gain_ref[:, n : n + wide]
        for t in range(y.shape[1] // LANES):
            tile = n // LANES + t
            j = tile // tiles
            y_ref[tile] = y[:, t * LANES : (t + 1) * LANES]
            where = slice(block * rows, (block + 1) * rows)
            to = slice(tile % tiles * LANES, (tile % tiles + 1) * LANES)
            for i in range(items):
                outs[j][i, where, to] = y_ref[tile, pl.ds(i, rows, stride=items), :].astype(BF)

    chunks = rows // 4
    pending = []
    for block in range(blocks + 1):
        now, later = (xb_ref, xa_ref) if block % 2 == 0 else (xa_ref, xb_ref)
        if block < blocks:
            loads[block].wait()
        if block == 0:
            for c in range(chunks):
                norm_rows(0, later, c)
            for copy in weights:
                copy.wait()
            continue
        starts = list(range(0, 3 * width, wide))
        for at, n in enumerate(starts):
            y = dot(now[...], w_ref[:, n : min(n + wide, 3 * width)])
            if block < blocks:
                for c in range(at * chunks // len(starts), (at + 1) * chunks // len(starts)):
                    norm_rows(block, later, c)
            if pending:
                finish_tile(*pending.pop())
            pending.append((block - 1, n, y))
    finish_tile(*pending.pop())


def project(scalars, hidden, modulation, gains, w):
    row_total, items, width_d = hidden.shape
    width = w.shape[2]
    rows = 128
    blocks = row_total // rows
    out = pl.BlockSpec((items, row_total, width), lambda s, r: (0, 0, 0))
    grid_spec = pltpu.PrefetchScalarGridSpec(
        num_scalar_prefetch=1,
        grid=(1,),
        in_specs=[
            pl.BlockSpec(memory_space=pl.ANY),
            pl.BlockSpec((None, 3, items, width_d), lambda s, r: (r[4], 0, 0, 0)),
            pl.BlockSpec((1, 2 * width), lambda s, r: (0, 0)),
            pl.BlockSpec(memory_space=pl.ANY),
        ],
        out_specs=[out] * 3,
        scratch_shapes=[
            pltpu.VMEM((width_d, 3 * width), BF),
            pltpu.VMEM((blocks, rows, items, width_d), BF),
            pltpu.VMEM((rows * items, width_d), BF),
            pltpu.VMEM((rows * items, width_d), BF),
            pltpu.VMEM((8, width_d), F32),
            pltpu.VMEM((8, width_d), F32),
            pltpu.VMEM((3 * width // LANES, rows * items, LANES), F32),
            pltpu.SemaphoreType.DMA((blocks + 3,)),
        ],
    )
    return pl.pallas_call(
        project_kernel,
        grid_spec=grid_spec,
        out_shape=[jax.ShapeDtypeStruct((items, row_total, width), BF)] * 3,
        compiler_params=params(58),
        cost_estimate=COST,
        name="project",
    )(scalars, hidden, modulation, gains, w)


def half_masks():
    lane = lax.broadcasted_iota(jnp.int32, (8, LANES), 1)
    return [(lane < HEAD).astype(F32)[0:1].astype(BF), (lane >= HEAD).astype(F32)[0:1].astype(BF)]


def weigh(values, mask, valid=None):
    ones = jnp.broadcast_to(mask, values.shape)
    both = jnp.concatenate([values * mask, ones], axis=1)
    return both if valid is None else both * valid


def sums_tile(sums):
    rows = sums.shape[0]
    r = lax.broadcasted_iota(jnp.int32, (rows, LANES), 0)
    c = lax.broadcasted_iota(jnp.int32, (rows, LANES), 1) % HEAD
    line = jnp.sum(jnp.where(r == c, sums, 0.0), axis=0, keepdims=True)
    high = line.astype(BF).astype(F32)
    low = line - high
    at = lax.broadcasted_iota(jnp.int32, (8, LANES), 0)
    return jnp.where(at == 0, high, jnp.where(at == 1, low, 0.0)).astype(BF)


def own_kernel(s_ref, q_ref, k_ref, v_ref, *refs):
    out_refs, part_ref, sums_ref = refs[:PATCHES], refs[PATCHES], refs[PATCHES + 1]
    rows, width = q_ref.shape
    share = rows // PATCHES
    masks = half_masks()
    for t in range(width // LANES):
        lanes = slice(t * LANES, (t + 1) * LANES)
        kp, vp, qp = k_ref[:, lanes], v_ref[:, lanes], q_ref[:, lanes]
        acc = None
        for h in range(2):
            p = jnp.exp(lax.dot_general(qp * masks[h], kp, NT, preferred_element_type=F32)).astype(BF)
            term = dot(p, weigh(vp, masks[h]))
            acc = term if acc is None else acc + term
        sums = acc[:, LANES:]
        sums_ref[t] = sums
        part_ref[t] = acc[:, :LANES] / sums
        for g in range(PATCHES):
            at = pl.ds(pl.multiple_of((s_ref[7] ^ g) * share, share), share)
            out_refs[g][0:share, lanes] = part_ref[t, at, :].astype(BF)
            out_refs[g][share : share + 8, lanes] = sums_tile(sums_ref[t, at, :])


def own_attention(scalars, q, k, v):
    items, rows, width = k.shape
    share = rows // PATCHES
    grid_spec = pltpu.PrefetchScalarGridSpec(
        num_scalar_prefetch=1,
        grid=(items,),
        in_specs=[pl.BlockSpec((None, rows, width), lambda s, r: (s, 0, 0))] * 3,
        out_specs=[pl.BlockSpec((None, share + 8, width), lambda s, r: (s, 0, 0))] * PATCHES,
        scratch_shapes=[pltpu.VMEM((width // LANES, rows, LANES), F32)] * 2,
    )
    return pl.pallas_call(
        own_kernel,
        grid_spec=grid_spec,
        out_shape=[jax.ShapeDtypeStruct((items, share + 8, width), BF)] * PATCHES,
        compiler_params=params(58),
        cost_estimate=COST,
        name="own",
    )(scalars, q, k, v)


def remote_kernel(s_ref, *refs):
    q_refs, kv_refs = refs[0:PATCHES], refs[PATCHES : 2 * PATCHES]
    out_ref, w_ref, text_ref = refs[2 * PATCHES :]
    rows = q_refs[0].shape[0]
    trows = kv_refs[0].shape[1] - rows
    share = rows // PATCHES
    patch, length = s_ref[5], s_ref[6]
    masks = half_masks()
    text_ref[...] = jnp.zeros_like(text_ref)
    position = lax.broadcasted_iota(jnp.int32, (rows, 2 * LANES), 0)
    good = position < 0
    for o in range(PATCHES):
        for j in range(2):
            text_ref[j, o * trows : (o + 1) * trows] = kv_refs[o][j, rows:].astype(F32)
        owner = lax.rem(patch - o + PATCHES, PATCHES)
        here = (position >= o * trows) & (position < (o + 1) * trows)
        good = good | (here & (position - o * trows + owner * trows < length))
    valid = good.astype(F32).astype(BF)
    text_k, text_v = text_ref[0].astype(BF), text_ref[1].astype(BF)
    for h in range(2):
        for o in range(PATCHES):
            w_ref[h, o] = weigh(kv_refs[o][1, 0:rows], masks[h])
        w_ref[h, PATCHES] = weigh(text_v, masks[h], valid)
    for o in range(PATCHES):
        qp = q_refs[o][...]
        acc = None
        for h in range(2):
            qh = qp * masks[h]
            for c in range(PATCHES + 1):
                if c == o:
                    continue
                keys = text_k if c == PATCHES else kv_refs[c][0, 0:rows]
                p = jnp.exp(lax.dot_general(qh, keys, NT, preferred_element_type=F32)).astype(BF)
                term = dot(p, w_ref[h, c])
                acc = term if acc is None else acc + term
        sums = acc[:, LANES:]
        part = (acc[:, :LANES] / sums).astype(BF)
        base = lax.rem(patch - o + PATCHES, PATCHES) * PATCHES
        for u in range(PATCHES):
            out_ref[base + u, 0:share] = part[u * share : (u + 1) * share]
            out_ref[base + u, share : share + 8] = sums_tile(sums[u * share : (u + 1) * share])


def remote_attention(scalars, q, far_qs, kvs):
    _, rows, width = q.shape
    total = kvs[0].shape[1]
    share = rows // PATCHES
    grid_spec = pltpu.PrefetchScalarGridSpec(
        num_scalar_prefetch=1,
        grid=(width // LANES,),
        in_specs=[pl.BlockSpec((None, rows, LANES), lambda s, r: (r[5], 0, s))]
        + [pl.BlockSpec((rows, LANES), lambda s, r: (0, s))] * (PATCHES - 1)
        + [pl.BlockSpec((2, total, LANES), lambda s, r: (0, 0, s))] * PATCHES,
        out_specs=pl.BlockSpec((PATCHES * PATCHES, share + 8, LANES), lambda s, r: (0, 0, s)),
        scratch_shapes=[
            pltpu.VMEM((2, PATCHES + 1, rows, 2 * LANES), BF),
            pltpu.VMEM((2, rows, LANES), F32),
        ],
    )
    return pl.pallas_call(
        remote_kernel,
        grid_spec=grid_spec,
        out_shape=jax.ShapeDtypeStruct((PATCHES * PATCHES, share + 8, width), BF),
        compiler_params=params(58),
        cost_estimate=COST,
        name="remote",
    )(scalars, q, *far_qs, *kvs)


def spread(lines, ones2):
    r = lax.broadcasted_iota(jnp.int32, (HEAD, LANES), 0)
    c = lax.broadcasted_iota(jnp.int32, (HEAD, LANES), 1) % HEAD
    parts = []
    for line in lines:
        f = line.astype(F32)
        parts.append(
            jnp.concatenate(
                [jnp.where(r == c, f[0:1], 0.0), jnp.where(r == c, f[1:2], 0.0)], axis=1
            ).astype(BF)
        )
    return dot(jnp.concatenate(parts, axis=0), ones2)


def finish_kernel(s_ref, far_ref, near0, near1, near2, near3, hidden_ref, mod_ref, w0, w1, w2, w3, out_ref, acc_ref):
    nears, ws = [near0, near1, near2, near3], [w0, w1, w2, w3]
    share, items, width_d = hidden_ref.shape
    rows = share * items
    width = w0.shape[0]
    ones2 = block_ones(2 * LANES)
    a = lax.broadcasted_iota(jnp.int32, (rows, rows), 0)
    b = lax.broadcasted_iota(jnp.int32, (rows, rows), 1)
    order = ((a % items) * share + a // items == b).astype(F32).astype(BF)
    tp = s_ref[7]
    for g in range(4):
        source = tp ^ g
        mixed = []
        for t in range(width // LANES):
            lanes = slice(t * LANES, (t + 1) * LANES)
            far = [far_ref[i, source, :, lanes] for i in range(items)]
            near = [nears[g][i, :, lanes] for i in range(items)]
            sums = [spread([x[share:] for x in part], ones2) for part in (far, near)]
            values = [
                jnp.concatenate([x[:share] for x in part], axis=0).astype(F32) for part in (far, near)
            ]
            total = values[0] * sums[0] + values[1] * sums[1]
            mixed.append((total / (sums[0] + sums[1])).astype(BF))
        joined = dot(order, jnp.concatenate(mixed, axis=1)).astype(BF)
        for n in range(0, width_d, 256):
            lanes = slice(n, min(n + 256, width_d))
            term = dot(joined, ws[g][:, lanes]).astype(BF).astype(F32)
            if g == 0:
                acc_ref[:, lanes] = term
            else:
                acc_ref[:, lanes] += term
    gate = mod_ref[2].astype(F32)
    gate = jnp.concatenate([gate, gate], axis=0)

    def last(c, carry):
        at = pl.multiple_of(c * 16, 16)
        own = hidden_ref[pl.ds(c * 4, 4)].reshape(16, width_d).astype(F32).reshape(2, 8, width_d)
        new = own + gate[None] * acc_ref[pl.ds(at, 16), :].reshape(2, 8, width_d)
        out_ref[pl.ds(c * 4, 4)] = new.reshape(16, width_d).astype(BF).reshape(4, items, width_d)
        return carry

    lax.fori_loop(0, rows // 16, last, 0, unroll=4)


def finish(scalars, far, near, hidden, modulation, ws):
    row_total, items, width_d = hidden.shape
    share = row_total // PATCHES
    width = ws[0].shape[0]
    grid_spec = pltpu.PrefetchScalarGridSpec(
        num_scalar_prefetch=1,
        grid=(1,),
        in_specs=[pl.BlockSpec((items, 4, share + 8, width), lambda s, r: (0, 0, 0, 0))]
        + [pl.BlockSpec((items, share + 8, width), lambda s, r: (0, 0, 0))] * 4
        + [
            pl.BlockSpec((share, items, width_d), lambda s, r: (r[7], 0, 0)),
            pl.BlockSpec((None, 3, items, width_d), lambda s, r: (r[4], 0, 0, 0)),
        ]
        + [pl.BlockSpec(memory_space=pltpu.VMEM)] * 4,
        out_specs=pl.BlockSpec((share, items, width_d), lambda s, r: (0, 0, 0)),
        scratch_shapes=[
            pltpu.VMEM((share * items, width_d), F32),
        ],
    )
    return pl.pallas_call(
        finish_kernel,
        grid_spec=grid_spec,
        out_shape=jax.ShapeDtypeStruct((share, items, width_d), BF),
        compiler_params=params(58),
        cost_estimate=COST,
        name="finish",
    )(scalars, far, *near, hidden, modulation, *ws)


def body(layout, hidden, modulation, w_qkv, w_out, qk_gain, stale_kv, text_kv, text_len):
    slots, tps, groups, w_pairs, core_pairs = layout
    place = lax.axis_index("req")
    tp = lax.axis_index("tp")
    group = place % groups
    patch = place // groups
    items_at = [(patch + o) % PATCHES for o in range(PATCHES)]
    length = lax.dynamic_slice(text_len, (group, patch), (1, 1))[0, 0]
    scalars = jnp.stack([v.astype(jnp.int32) for v in items_at + [group, patch, length, tp]])
    both = ("req", "tp")
    local_heads = w_out.shape[0] // HEAD

    columns = [[g + groups * p for p in range(PATCHES)] for g in range(groups)]
    rings = [[place * tps + t for place in column for t in range(tps)] for column in columns]

    def along_x(value, by):
        return lax.ppermute(value, "req", [(i, (i + by * groups) % slots) for i in range(slots)])

    packed = [pack(items_at[o].astype(jnp.int32)[None], stale_kv[0], text_kv[0]) for o in range(PATCHES)]
    *packed, scalars = lax.optimization_barrier((*packed, scalars))
    kvs = [packed[0]] + [along_x(packed[o], o) for o in (1, 2, 3)]
    w_far = lax.ppermute(w_out, both, w_pairs)
    w_near = lax.ppermute(w_out, both, core_pairs)
    mod = jnp.transpose(modulation, (0, 2, 1, 3))
    gains = jnp.concatenate([qk_gain[0] * 0.125] * local_heads + [qk_gain[1]] * local_heads)[None]
    q, k, v = project(scalars, hidden[0], mod, gains, jnp.transpose(w_qkv, (1, 0, 2)))
    owns = own_attention(scalars, q, k, v)
    pieces = [lax.dynamic_index_in_dim(q, items_at[o], 0, keepdims=False) for o in range(1, PATCHES)]
    pieces, kvs, owns = lax.optimization_barrier((pieces, kvs, owns))
    far_qs = [along_x(pieces[o - 1], o) for o in range(1, PATCHES)]
    w_across = lax.ppermute(w_far, both, core_pairs)
    near = [owns[0]] + [
        lax.ppermute(owns[g], "tp", [(i, i ^ g) for i in range(tps)]) for g in range(1, tps)
    ]
    sent = remote_attention(scalars, q, far_qs, kvs)
    far = lax.all_to_all(sent, both, 0, 0, axis_index_groups=rings, tiled=True)
    far = far.reshape(PATCHES, tps, *far.shape[1:])
    fresh = jnp.transpose(jnp.stack([k, v], axis=0), (2, 1, 0, 3))
    updated = finish(scalars, far, near, hidden[0], mod, [w_out, w_near, w_far, w_across])
    return (updated[None], fresh[None])


def solution(mesh):
    slots, tps = mesh.shape["req"], mesh.shape["tp"]
    groups = slots // PATCHES
    ring = 8
    w_pairs = []
    for place in range(slots):
        column, high = place // (ring // 2), place % (ring // 2)
        for t in range(tps):
            low, core = t // 2, t % 2
            z = (2 * high + low + (1 if core else -1)) % ring
            target = column * (ring // 2) + z // 2
            w_pairs.append((place * tps + t, target * tps + z % 2 * 2 + core))
    core_pairs = [(i, i ^ 1) for i in range(slots * tps)]
    layout = (slots, tps, groups, w_pairs, core_pairs)
    return jax.shard_map(
        functools.partial(body, layout),
        mesh=mesh,
        in_specs=(
            P("req", None, None, None),
            P(),
            P(None, None, "tp"),
            P("tp", None),
            P(),
            P("req", None, None, None, "tp"),
            P("req", None, None, None, "tp"),
            P(),
        ),
        out_specs=(P("req", "tp", None, None), P("req", None, None, None, "tp")),
        check_vma=False,
    )
```

time: 218 us -> 114 us (0.52)
  Pallas kernels: 0 us -> 54.7 us
  waiting for transfers between devices: 79.6 us -> 25.4 us
  local copies, waits for them, and re-layouts: 51.9 us -> 9.13 us
  matrix products: 37.4 us -> 0 us
  other arithmetic: 23 us -> 0.18 us
  between operations: 14.3 us -> 0.81 us
  starting transfers between devices: 10.6 us -> 23.5 us
    pallas_call x0 -> x8, Pallas kernels: none -> 54.7 us  [the longest x1 15.8 us: project(): pl.pallas_call(project_kernel, grid_spec=grid_spec, out_shape=[jax.ShapeD...]
    reduce_scatter x1 -> x0, waiting for transfers between devices: 51.7 us -> none  [body(): lax.psum_scatter(jnp.einsum('rbe,ed->rbd', mixed, w_out, preferred_elemen...]
    dot_general x4 -> x0, matrix products: 37.4 us -> none  [the longest x1 14 us: attend(): jnp.einsum('rbhe,kbhe->bhrk', query_heads, key_heads, preferred_element_t...]
    unnamed x21 -> x35, local copies, waits for them, and re-layouts: 23.8 us -> 4.84 us
    concatenate x2 -> x1, local copies, waits for them, and re-layouts: 12.6 us -> 0.08 us  [body(): jnp.concatenate([qk_gain[0] * 0.125] * local_heads + [qk_gain[1]] * local...]
    reduce_sum x4 -> x0, other arithmetic: 10.7 us -> none  [the longest x1 5.79 us: modulate(): variance = jnp.mean(center * center, axis=-1, keepdims=True)]
    ppermute x6 -> x12, starting transfers between devices: 10.6 us -> 18.4 us  [the longest x6 7.92 us: along_x(): lax.ppermute(value, 'req', [(i, (i + by * groups) % slots) for i in range...]
    convert_element_type x4 -> x0, other arithmetic: 7.55 us -> none  [the longest x1 6.59 us: modulate(): return (normed * (1.0 + scale_rows) + shift_rows).astype(jnp.bfloat16)]
  transfers between devices with their start and end apart: 7 -> 13, of which waited for: 2 -> 4; matrix products, arithmetic and copies ran while one was open for 25% -> 6% of each run, Pallas kernels for 0% -> 39%
where the time goes in v1:
time: 114 us
  Pallas kernels  54.7 us (48%)
  waiting for transfers between devices  25.4 us (22%)
  starting transfers between devices  23.5 us (21%)
  local copies, waits for them, and re-layouts  9.13 us (8%)
    ppermute x3, waiting for transfers between devices, body(): lax.ppermute(owns[g], 'tp', [(i, i ^ g) for i in range(tps)])  16.4 us
    pallas_call x1, Pallas kernels, project(): pl.pallas_call(project_kernel, grid_spec=grid_spec, out_shape=[jax.ShapeD...  15.8 us
    pallas_call x4, Pallas kernels, pack(): pl.pallas_call(pack_kernel, grid_spec=grid_spec, out_shape=jax.ShapeDtype...  11.4 us
    pallas_call x1, Pallas kernels, finish(): pl.pallas_call(finish_kernel, grid_spec=grid_spec, out_shape=jax.ShapeDty...  10.9 us
    pallas_call x1, Pallas kernels, remote_attention(): pl.pallas_call(remote_kernel, grid_spec=grid_spec, out_shape=jax.ShapeDty...  10.5 us
    ppermute x6, waiting for transfers between devices, along_x(): lax.ppermute(value, 'req', [(i, (i + by * groups) % slots) for i in range...  8.95 us
    ppermute x6, starting transfers between devices, along_x(): lax.ppermute(value, 'req', [(i, (i + by * groups) % slots) for i in range...  7.92 us
    pallas_call x1, Pallas kernels, own_attention(): pl.pallas_call(own_kernel, grid_spec=grid_spec, out_shape=[jax.ShapeDtype...  6.11 us
  transfers between devices with their start and end apart: 13, of which 4 were waited for; matrix products, arithmetic and copies ran while one was open for 6% of the time, Pallas kernels for 39%

profile of v1, /device:TPU:1, one launch (start us, length us, event | category | flops | bytes accessed | tf_op | source)
XLA Modules:
  0.0 113.8 jit_solution(15898175471926259910)
XLA Ops:
  0.6 2.5 %collective-permute-start.10 = (bf16[384,2432]{1,0:T(8,128)(2,1)}, bf16[384,2432]{1,0:T(8,128)(2,1)}, u32[]{:S(2)}, u32[]{:S(2)}) collective-permute-start(bf16[384,2432]{1,0:T(8,128)(2,1)} %w0.1), channel_id=1, source_target_pairs={{0,14},{1,3},{2,0},{3,5},{4,2},{5,7},{6,4},{7,9},{8,6},{9,11},{10,... | collective-permute-start | bytes 5603336 | tf_op jit(solution)/shard_map/ppermute | solution.py:418
  3.2 2.8 %pack.5 = bf16[2,296,384]{2,1,0:T(8,128)(2,1)} custom-call(s32[1]{0:T(128)} %bitcast.3.item_ref, bf16[256,4,2,384]{3,2,1,0:T(2,128)(2,1)} %bitcast.31, bf16[40,4,2,384]{3,2,1,0:T(2,128)(2,1)} %bitcast.38), custom_call_target="tpu_custom_call" | custom-call | flops 1000 | bytes 1000 | tf_op jit(solution)/shard_map/pack/pallas_call | solution.py:58
  6.0 2.8 %pack.6 = bf16[2,296,384]{2,1,0:T(8,128)(2,1)} custom-call(s32[1]{0:T(128)} %bitcast.4.item_ref, bf16[256,4,2,384]{3,2,1,0:T(2,128)(2,1)} %bitcast.32, bf16[40,4,2,384]{3,2,1,0:T(2,128)(2,1)} %bitcast.39), custom_call_target="tpu_custom_call" | custom-call | flops 1000 | bytes 1000 | tf_op jit(solution)/shard_map/pack/pallas_call | solution.py:58
  8.8 2.8 %pack.7 = bf16[2,296,384]{2,1,0:T(8,128)(2,1)} custom-call(s32[1]{0:T(128)} %bitcast.5.item_ref, bf16[256,4,2,384]{3,2,1,0:T(2,128)(2,1)} %bitcast.33, bf16[40,4,2,384]{3,2,1,0:T(2,128)(2,1)} %bitcast.40), custom_call_target="tpu_custom_call" | custom-call | flops 1000 | bytes 1000 | tf_op jit(solution)/shard_map/pack/pallas_call | solution.py:58
  11.7 2.9 %pack.4.refs_4_ = bf16[2,296,384]{2,1,0:T(8,128)(2,1)} custom-call(s32[1]{0:T(128)} %bitcast.item_ref, bf16[256,4,2,384]{3,2,1,0:T(2,128)(2,1)} %bitcast.34, bf16[40,4,2,384]{3,2,1,0:T(2,128)(2,1)} %bitcast.41), custom_call_target="tpu_custom_call" | custom-call | flops 1000 | bytes 1000 | tf_op jit(solution)/shard_map/pack/pallas_call | solution.py:58
  14.6 1.3 %dynamic_slice.13 = s32[1,1]{0,1:T(1,128)} dynamic-slice(s32[16,4]{0,1:T(4,128)} %param.15, s32[]{:T(128)S(6)} %select_n.49, s32[]{:T(128)S(6)} %select_n.50), dynamic_slice_sizes={1,1} | dynamic-slice | bytes 12 | tf_op jit(solution)/shard_map/dynamic_slice | solution.py:404
  15.8 1.2 %stack.28.s_ref = s32[8]{0:T(128)} concatenate(s32[1]{0:T(128)} %bitcast.item_ref, s32[1]{0:T(128)} %bitcast.3.item_ref, s32[1]{0:T(128)} %bitcast.4.item_ref, s32[1]{0:T(128)} %bitcast.5.item_ref, s32[1]{0:T(128)} %bitcast.6, s32[1]{0:T(128)} %bitcast.7, s32[1]{0:T(128)} %bitcast.8, s32[1]{0:T(128)} %bitcast.9), dimensions={0} | concatenate | bytes 64 | tf_op jit(solution)/shard_map/stack | solution.py:405
  17.0 1.2 %collective-permute-start = (bf16[2,296,384]{2,1,0:T(8,128)(2,1)S(1)}, bf16[2,296,384]{2,1,0:T(8,128)(2,1)S(1)}, u32[]{:S(2)}, u32[]{:S(2)}) collective-permute-start(bf16[2,296,384]{2,1,0:T(8,128)(2,1)S(1)} %copy-done.3), channel_id=1, source_target_pairs={{0,64},{4,68},{8,72},{12,76},{16,80},{20,84},{24,88},{28,92},{32,9... | collective-permute-start | bytes 1363976 | tf_op jit(solution)/shard_map/ppermute | solution.py:413
  18.2 2.5 %collective-permute-start.1 = (bf16[2,296,384]{2,1,0:T(8,128)(2,1)S(1)}, bf16[2,296,384]{2,1,0:T(8,128)(2,1)S(1)}, u32[]{:S(2)}, u32[]{:S(2)}) collective-permute-start(bf16[2,296,384]{2,1,0:T(8,128)(2,1)S(1)} %copy-done.4), channel_id=1, source_target_pairs={{0,128},{4,132},{8,136},{12,140},{16,144},{20,148},{24,152},{28,15... | collective-permute-start | bytes 1363976 | tf_op jit(solution)/shard_map/ppermute | solution.py:413
  20.7 1.2 %collective-permute-start.2 = (bf16[2,296,384]{2,1,0:T(8,128)(2,1)S(1)}, bf16[2,296,384]{2,1,0:T(8,128)(2,1)S(1)}, u32[]{:S(2)}, u32[]{:S(2)}) collective-permute-start(bf16[2,296,384]{2,1,0:T(8,128)(2,1)S(1)} %copy-done.5), channel_id=1, source_target_pairs={{0,192},{4,196},{8,200},{12,204},{16,208},{20,212},{24,216},{28,22... | collective-permute-start | bytes 1363976 | tf_op jit(solution)/shard_map/ppermute | solution.py:413
  21.9 5.7 %collective-permute-start.9 = (bf16[384,2432]{1,0:T(8,128)(2,1)}, bf16[384,2432]{1,0:T(8,128)(2,1)}, u32[]{:S(2)}, u32[]{:S(2)}) collective-permute-start(bf16[384,2432]{1,0:T(8,128)(2,1)} %w0.1), channel_id=1, source_target_pairs={{0,1},{1,0},{2,3},{3,2},{4,5},{5,4},{6,7},{7,6},{8,9},{9,8},{10,11... | collective-permute-start | bytes 5603336 | tf_op jit(solution)/shard_map/ppermute | solution.py:419
  27.7 0.6 broadcast_in_dim.25.gain_ref
  28.3 15.8 %project.1 = (bf16[4,256,384]{2,1,0:T(8,128)(2,1)}, bf16[4,256,384]{2,1,0:T(8,128)(2,1)}, bf16[4,256,384]{2,1,0:T(8,128)(2,1)}) custom-call(s32[8]{0:T(128)} %stack.28.s_ref, bf16[256,4,2432]{2,1,0:T(4,128)(2,1)} %bitcast.35, bf16[16,3,4,2432]{3,2,1,0:T(4,128)(2,1)} %bitcast.42, f32[1,768]{1,0:T(1,128)} %broadcast_in_dim.25.gain_ref, ...), custom_call_target="tpu_custom_call" | custom-call | flops 1000 | bytes 1000 | tf_op jit(solution)/shard_map/project/pallas_call | solution.py:167
  44.2 1.2 %dynamic-slice_bitcast_fusion = (bf16[256,384]{1,0:T(8,128)(2,1)S(1)}, bf16[256,384]{1,0:T(8,128)(2,1)S(1)}, bf16[256,384]{1,0:T(8,128)(2,1)S(1)}) fusion(bf16[4,256,384]{2,1,0:T(8,128)(2,1)} %get-tuple-element.26.q_ref.refs_0_, s32[]{:T(128)S(6)} %select_n.53, s32[]{:T(128)S(6)} %select_n.52, s32[]{:T(128)S(6)} %select_n.51), kind=kLoop, calls=%fused_computation.1 | loop fusion | bytes 1179660 | tf_op jit(solution)/shard_map/jit(dynamic_index_in_dim)/squeeze | solution.py:424
  45.4 6.1 %own.1 = (bf16[4,72,384]{2,1,0:T(8,128)(2,1)}, bf16[4,72,384]{2,1,0:T(8,128)(2,1)}, bf16[4,72,384]{2,1,0:T(8,128)(2,1)}, bf16[4,72,384]{2,1,0:T(8,128)(2,1)}) custom-call(s32[8]{0:T(128)} %stack.28.s_ref, bf16[4,256,384]{2,1,0:T(8,128)(2,1)} %get-tuple-element.26.q_ref.refs_0_, bf16[4,256,384]{2,1,0:T(8,128)(2,1)} %get-tuple-element.31.k_ref, ...), custom_call_target="tpu_custom_call" | custom-call | flops 1000 | bytes 1000 | tf_op jit(solution)/shard_map/own/pallas_call | solution.py:231
  51.6 0.6 collective-permute-start.3
  52.2 0.6 collective-permute-start.4
  52.8 1.9 %collective-permute-start.5 = (bf16[256,384]{1,0:T(8,128)(2,1)S(1)}, bf16[256,384]{1,0:T(8,128)(2,1)S(1)}, u32[]{:S(2)}, u32[]{:S(2)}) collective-permute-start(bf16[256,384]{1,0:T(8,128)(2,1)S(1)} %get-tuple-element.39), channel_id=1, source_target_pairs={{0,192},{4,196},{8,200},{12,204},{16,208},{20,212},{24,216},{28,22... | collective-permute-start | bytes 589832 | tf_op jit(solution)/shard_map/ppermute | solution.py:413
  54.7 8.6 %collective-permute-done.3.refs_1_ = bf16[256,384]{1,0:T(8,128)(2,1)S(1)} collective-permute-done((bf16[256,384]{1,0:T(8,128)(2,1)S(1)}, bf16[256,384]{1,0:T(8,128)(2,1)S(1)}, u32[]{:S(2)}, u32[]{:S(2)}) %collective-permute-start.3) | collective-permute-done | bytes 196640 | tf_op jit(solution)/shard_map/ppermute | solution.py:413
  63.3 0.3 collective-permute-done.5.refs_3_
  63.7 0.3 copy-done.12
  64.1 0.7 copy-done.14
  64.7 10.5 %remote.1 = bf16[16,72,384]{2,1,0:T(8,128)(2,1)} custom-call(s32[8]{0:T(128)} %stack.28.s_ref, bf16[4,256,384]{2,1,0:T(8,128)(2,1)} %get-tuple-element.26.q_ref.refs_0_, bf16[256,384]{1,0:T(8,128)(2,1)} %copy-done.12, bf16[256,384]{1,0:T(8,128)(2,1)} %copy-done.13, bf16[256,384]{1,0:T(8,128)(2,1)} %copy-done.14, bf16[2,296,384]{2,1,0:T(8,128)(2,1)} %pack.4.refs_4_, ...), custom_call_target="tpu_custom_call" | custom-call | flops 1000 | bytes 1000 | tf_op jit(solution)/shard_map/remote/pallas_call | solution.py:300
  75.3 5.1 %all-to-all-start = ((bf16[16,72,384]{2,1,0:T(8,128)(2,1)}), bf16[16,72,384]{2,1,0:T(8,128)(2,1)S(1)}, u32[]{:S(2)}, u32[]{:S(2)}) async-start(bf16[16,72,384]{2,1,0:T(8,128)(2,1)} %remote.1), calls=%async_computation | async-start | bytes 1769472 | tf_op jit(solution)/shard_map/all_to_all | solution.py:432
  80.6 1.6 %collective-permute-start.7 = (bf16[4,72,384]{2,1,0:T(8,128)(2,1)}, bf16[4,72,384]{2,1,0:T(8,128)(2,1)S(1)}, u32[]{:S(2)}, u32[]{:S(2)}) collective-permute-start(bf16[4,72,384]{2,1,0:T(8,128)(2,1)} %get-tuple-element.46), channel_id=1, source_target_pairs={{0,2},{1,3},{2,0},{3,1},{4,6},{5,7},{6,4},{7,5},{8,10},{9,11},{10,... | collective-permute-start | bytes 663560 | tf_op jit(solution)/shard_map/ppermute | solution.py:429
  82.1 0.4 collective-permute-start.8
  82.7 2.8 %copy.10 = bf16[1,256,4,2,384]{4,3,2,1,0:T(2,128)(2,1)} copy(bf16[1,256,4,2,384]{4,1,2,3,0:T(8,128)(2,1)S(1)} %maximum_bitcast_fusion) | data formatting | bytes 3145728
  85.5 11.5 %collective-permute-done.7.near2 = bf16[4,72,384]{2,1,0:T(8,128)(2,1)S(1)} collective-permute-done((bf16[4,72,384]{2,1,0:T(8,128)(2,1)}, bf16[4,72,384]{2,1,0:T(8,128)(2,1)S(1)}, u32[]{:S(2)}, u32[]{:S(2)}) %collective-permute-start.7) | collective-permute-done | bytes 221216 | tf_op jit(solution)/shard_map/ppermute | solution.py:429
  97.0 4.9 %collective-permute-done.8.near3 = bf16[4,72,384]{2,1,0:T(8,128)(2,1)S(1)} collective-permute-done((bf16[4,72,384]{2,1,0:T(8,128)(2,1)S(1)}, bf16[4,72,384]{2,1,0:T(8,128)(2,1)S(1)}, u32[]{:S(2)}, u32[]{:S(2)}) %collective-permute-start.8) | collective-permute-done | bytes 221216 | tf_op jit(solution)/shard_map/ppermute | solution.py:429
  102.0 0.6 copy-done.11
  102.6 0.3 copy-done
  102.9 10.9 %finish.1 = bf16[64,4,2432]{2,1,0:T(4,128)(2,1)} custom-call(s32[8]{0:T(128)} %stack.28.s_ref, bf16[4,4,72,384]{3,2,1,0:T(8,128)(2,1)} %bitcast.44, bf16[4,72,384]{2,1,0:T(8,128)(2,1)} %get-tuple-element.44.near0, bf16[4,72,384]{2,1,0:T(8,128)(2,1)} %copy-done.9, bf16[4,72,384]{2,1,0:T(8,128)(2,1)} %copy-done.10, bf16[4,72,384]{2,1,0:T(8,128)(2,1)} %copy-done.11, ...), custom_call_target="tpu_custom_call" | custom-call | flops 1000 | bytes 1000 | tf_op jit(solution)/shard_map/finish/pallas_call | solution.py:387
  (44 shorter events, 0.7 us)
Async XLA Ops:
  0.6 43.5 %collective-permute-start.10 = (bf16[384,2432]{1,0:T(8,128)(2,1)}, bf16[384,2432]{1,0:T(8,128)(2,1)}, u32[]{:S(2)}, u32[]{:S(2)}) collective-permute-start(bf16[384,2432]{1,0:T(8,128)(2,1)} %w0.1), channel_id=1, source_target_pairs={{0,14},{1,3},{2,0},{3,5},{4,2},{5,7},{6,4},{7,9},{8,6},{9,11},{10,... | collective-permute-start | bytes 5603336 | tf_op jit(solution)/shard_map/ppermute | solution.py:418
  11.6 5.4 %copy-start.3 = (bf16[2,296,384]{2,1,0:T(8,128)(2,1)S(1)}, bf16[2,296,384]{2,1,0:T(8,128)(2,1)}, u32[]{:S(2)}) copy-start(bf16[2,296,384]{2,1,0:T(8,128)(2,1)} %pack.5) | copy-start | bytes 1363972
  11.6 6.6 %copy-start.4 = (bf16[2,296,384]{2,1,0:T(8,128)(2,1)S(1)}, bf16[2,296,384]{2,1,0:T(8,128)(2,1)}, u32[]{:S(2)}) copy-start(bf16[2,296,384]{2,1,0:T(8,128)(2,1)} %pack.6) | copy-start | bytes 1363972
  11.6 9.1 %copy-start.5 = (bf16[2,296,384]{2,1,0:T(8,128)(2,1)S(1)}, bf16[2,296,384]{2,1,0:T(8,128)(2,1)}, u32[]{:S(2)}) copy-start(bf16[2,296,384]{2,1,0:T(8,128)(2,1)} %pack.7) | copy-start | bytes 1363972
  11.6 16.0 %copy-start.15 = (f32[2,64]{1,0:T(2,128)S(1)}, f32[2,64]{1,0:T(2,128)}, u32[]{:S(2)}) copy-start(f32[2,64]{1,0:T(2,128)} %param.12) | copy-start | bytes 1540
  17.0 34.5 %collective-permute-start = (bf16[2,296,384]{2,1,0:T(8,128)(2,1)S(1)}, bf16[2,296,384]{2,1,0:T(8,128)(2,1)S(1)}, u32[]{:S(2)}, u32[]{:S(2)}) collective-permute-start(bf16[2,296,384]{2,1,0:T(8,128)(2,1)S(1)} %copy-done.3), channel_id=1, source_target_pairs={{0,64},{4,68},{8,72},{12,76},{16,80},{20,84},{24,88},{28,92},{32,9... | collective-permute-start | bytes 1363976 | tf_op jit(solution)/shard_map/ppermute | solution.py:413
  18.2 33.3 %collective-permute-start.1 = (bf16[2,296,384]{2,1,0:T(8,128)(2,1)S(1)}, bf16[2,296,384]{2,1,0:T(8,128)(2,1)S(1)}, u32[]{:S(2)}, u32[]{:S(2)}) collective-permute-start(bf16[2,296,384]{2,1,0:T(8,128)(2,1)S(1)} %copy-done.4), channel_id=1, source_target_pairs={{0,128},{4,132},{8,136},{12,140},{16,144},{20,148},{24,152},{28,15... | collective-permute-start | bytes 1363976 | tf_op jit(solution)/shard_map/ppermute | solution.py:413
  20.7 30.9 %collective-permute-start.2 = (bf16[2,296,384]{2,1,0:T(8,128)(2,1)S(1)}, bf16[2,296,384]{2,1,0:T(8,128)(2,1)S(1)}, u32[]{:S(2)}, u32[]{:S(2)}) collective-permute-start(bf16[2,296,384]{2,1,0:T(8,128)(2,1)S(1)} %copy-done.5), channel_id=1, source_target_pairs={{0,192},{4,196},{8,200},{12,204},{16,208},{20,212},{24,216},{28,22... | collective-permute-start | bytes 1363976 | tf_op jit(solution)/shard_map/ppermute | solution.py:413
  21.9 80.1 %collective-permute-start.9 = (bf16[384,2432]{1,0:T(8,128)(2,1)}, bf16[384,2432]{1,0:T(8,128)(2,1)}, u32[]{:S(2)}, u32[]{:S(2)}) collective-permute-start(bf16[384,2432]{1,0:T(8,128)(2,1)} %w0.1), channel_id=1, source_target_pairs={{0,1},{1,0},{2,3},{3,2},{4,5},{5,4},{6,7},{7,6},{8,9},{9,8},{10,11... | collective-permute-start | bytes 5603336 | tf_op jit(solution)/shard_map/ppermute | solution.py:419
  44.1 57.8 %collective-permute-start.11 = (bf16[384,2432]{1,0:T(8,128)(2,1)}, bf16[384,2432]{1,0:T(8,128)(2,1)}, u32[]{:S(2)}, u32[]{:S(2)}) collective-permute-start(bf16[384,2432]{1,0:T(8,128)(2,1)} %collective-permute-done.10.w2), channel_id=1, source_target_pairs={{0,1},{1,0},{2,3},{3,2},{4,5},{5,4},{6,7},{7,6},{8,9},{9,8},{10,11... | collective-permute-start | bytes 5603336 | tf_op jit(solution)/shard_map/ppermute | solution.py:427
  51.5 12.1 %copy-start.6 = (bf16[2,296,384]{2,1,0:T(8,128)(2,1)}, bf16[2,296,384]{2,1,0:T(8,128)(2,1)S(1)}, u32[]{:S(2)}) copy-start(bf16[2,296,384]{2,1,0:T(8,128)(2,1)S(1)} %collective-permute-done.refs_5_) | copy-start | bytes 1363972
  51.6 12.1 %copy-start.7 = (bf16[2,296,384]{2,1,0:T(8,128)(2,1)}, bf16[2,296,384]{2,1,0:T(8,128)(2,1)S(1)}, u32[]{:S(2)}) copy-start(bf16[2,296,384]{2,1,0:T(8,128)(2,1)S(1)} %collective-permute-done.1.refs_6_) | copy-start | bytes 1363972
  51.6 12.1 %copy-start.8 = (bf16[2,296,384]{2,1,0:T(8,128)(2,1)}, bf16[2,296,384]{2,1,0:T(8,128)(2,1)S(1)}, u32[]{:S(2)}) copy-start(bf16[2,296,384]{2,1,0:T(8,128)(2,1)S(1)} %collective-permute-done.2.refs_7_) | copy-start | bytes 1363972
  51.6 11.7 %collective-permute-start.3 = (bf16[256,384]{1,0:T(8,128)(2,1)S(1)}, bf16[256,384]{1,0:T(8,128)(2,1)S(1)}, u32[]{:S(2)}, u32[]{:S(2)}) collective-permute-start(bf16[256,384]{1,0:T(8,128)(2,1)S(1)} %get-tuple-element.37), channel_id=1, source_target_pairs={{0,64},{4,68},{8,72},{12,76},{16,80},{20,84},{24,88},{28,92},{32,9... | collective-permute-start | bytes 589832 | tf_op jit(solution)/shard_map/ppermute | solution.py:413
  52.2 11.1 %collective-permute-start.4 = (bf16[256,384]{1,0:T(8,128)(2,1)S(1)}, bf16[256,384]{1,0:T(8,128)(2,1)S(1)}, u32[]{:S(2)}, u32[]{:S(2)}) collective-permute-start(bf16[256,384]{1,0:T(8,128)(2,1)S(1)} %get-tuple-element.38), channel_id=1, source_target_pairs={{0,128},{4,132},{8,136},{12,140},{16,144},{20,148},{24,152},{28,15... | collective-permute-start | bytes 589832 | tf_op jit(solution)/shard_map/ppermute | solution.py:413
  52.8 10.8 %collective-permute-start.5 = (bf16[256,384]{1,0:T(8,128)(2,1)S(1)}, bf16[256,384]{1,0:T(8,128)(2,1)S(1)}, u32[]{:S(2)}, u32[]{:S(2)}) collective-permute-start(bf16[256,384]{1,0:T(8,128)(2,1)S(1)} %get-tuple-element.39), channel_id=1, source_target_pairs={{0,192},{4,196},{8,200},{12,204},{16,208},{20,212},{24,216},{28,22... | collective-permute-start | bytes 589832 | tf_op jit(solution)/shard_map/ppermute | solution.py:413
  63.3 0.7 copy-start.12
  63.3 0.8 copy-start.13
  64.1 0.7 copy-start.14
  64.7 17.4 %copy-start.16 = (bf16[4,72,384]{2,1,0:T(8,128)(2,1)S(1)}, bf16[4,72,384]{2,1,0:T(8,128)(2,1)}, u32[]{:S(2)}) copy-start(bf16[4,72,384]{2,1,0:T(8,128)(2,1)} %get-tuple-element.47) | copy-start | bytes 663556
  75.2 7.3 %copy-start.1 = (bf16[4,256,384]{2,1,0:T(8,128)(2,1)S(1)}, bf16[4,256,384]{2,1,0:T(8,128)(2,1)}, u32[]{:S(2)}) copy-start(bf16[4,256,384]{2,1,0:T(8,128)(2,1)} %get-tuple-element.31.k_ref) | copy-start | bytes 2359300
  75.3 7.3 %copy-start.2 = (bf16[4,256,384]{2,1,0:T(8,128)(2,1)S(1)}, bf16[4,256,384]{2,1,0:T(8,128)(2,1)}, u32[]{:S(2)}) copy-start(bf16[4,256,384]{2,1,0:T(8,128)(2,1)} %get-tuple-element.32.v_ref) | copy-start | bytes 2359300
  75.3 26.7 %all-to-all-start = ((bf16[16,72,384]{2,1,0:T(8,128)(2,1)}), bf16[16,72,384]{2,1,0:T(8,128)(2,1)S(1)}, u32[]{:S(2)}, u32[]{:S(2)}) async-start(bf16[16,72,384]{2,1,0:T(8,128)(2,1)} %remote.1), calls=%async_computation | async-start | bytes 1769472 | tf_op jit(solution)/shard_map/all_to_all | solution.py:432
  80.4 5.1 %collective-permute-start.6 = (bf16[4,72,384]{2,1,0:T(8,128)(2,1)}, bf16[4,72,384]{2,1,0:T(8,128)(2,1)S(1)}, u32[]{:S(2)}, u32[]{:S(2)}) collective-permute-start(bf16[4,72,384]{2,1,0:T(8,128)(2,1)} %get-tuple-element.45), channel_id=1, source_target_pairs={{0,1},{1,0},{2,3},{3,2},{4,5},{5,4},{6,7},{7,6},{8,9},{9,8},{10,11... | collective-permute-start | bytes 663560 | tf_op jit(solution)/shard_map/ppermute | solution.py:429
  80.6 16.4 %collective-permute-start.7 = (bf16[4,72,384]{2,1,0:T(8,128)(2,1)}, bf16[4,72,384]{2,1,0:T(8,128)(2,1)S(1)}, u32[]{:S(2)}, u32[]{:S(2)}) collective-permute-start(bf16[4,72,384]{2,1,0:T(8,128)(2,1)} %get-tuple-element.46), channel_id=1, source_target_pairs={{0,2},{1,3},{2,0},{3,1},{4,6},{5,7},{6,4},{7,5},{8,10},{9,11},{10,... | collective-permute-start | bytes 663560 | tf_op jit(solution)/shard_map/ppermute | solution.py:429
  82.1 19.8 %collective-permute-start.8 = (bf16[4,72,384]{2,1,0:T(8,128)(2,1)S(1)}, bf16[4,72,384]{2,1,0:T(8,128)(2,1)S(1)}, u32[]{:S(2)}, u32[]{:S(2)}) collective-permute-start(bf16[4,72,384]{2,1,0:T(8,128)(2,1)S(1)} %copy-done.16), channel_id=1, source_target_pairs={{0,3},{1,2},{2,1},{3,0},{4,7},{5,6},{6,5},{7,4},{8,11},{9,10},{10,... | collective-permute-start | bytes 663560 | tf_op jit(solution)/shard_map/ppermute | solution.py:429
  85.5 16.5 %copy-start.9 = (bf16[4,72,384]{2,1,0:T(8,128)(2,1)}, bf16[4,72,384]{2,1,0:T(8,128)(2,1)S(1)}, u32[]{:S(2)}) copy-start(bf16[4,72,384]{2,1,0:T(8,128)(2,1)S(1)} %collective-permute-done.6.near1) | copy-start | bytes 663556
  97.0 5.0 %copy-start.10 = (bf16[4,72,384]{2,1,0:T(8,128)(2,1)}, bf16[4,72,384]{2,1,0:T(8,128)(2,1)S(1)}, u32[]{:S(2)}) copy-start(bf16[4,72,384]{2,1,0:T(8,128)(2,1)S(1)} %collective-permute-done.7.near2) | copy-start | bytes 663556
  101.9 0.7 copy-start.11
  101.9 1.0 copy-start

commit v2 on v1

v2 whole, which is shorter than its diff:
```python
import functools

import jax
import jax.numpy as jnp
from jax import lax
from jax.experimental import pallas as pl
from jax.experimental.pallas import tpu as pltpu
from jax.sharding import PartitionSpec as P

HEAD = 64
PATCHES = 4
EPSILON = 1e-06
LANES = 128
BF = jnp.bfloat16
F32 = jnp.float32
NT = (((1,), (1,)), ((), ()))
COST = pl.CostEstimate(flops=1000, bytes_accessed=1000, transcendentals=0)


def dot(a, b):
    return jnp.dot(a, b, preferred_element_type=F32)


def params(limit_mb, **kw):
    return pltpu.CompilerParams(vmem_limit_bytes=limit_mb << 20, **kw)


def split_bf(value):
    high = value.astype(BF)
    return high, (value - high.astype(F32)).astype(BF)


def block_ones(rows):
    a = lax.broadcasted_iota(jnp.int32, (rows, LANES), 0) % LANES // HEAD
    b = lax.broadcasted_iota(jnp.int32, (rows, LANES), 1) // HEAD
    return (a == b).astype(F32).astype(BF)


def project_kernel(s_ref, hidden_hbm, mod_ref, gain_ref, w_hbm, text_ref, q_hbm, k_ref, v_ref, *scratch):
    q_ref, hidden_ref, w_ref, xa_ref, xb_ref, scale_ref, shift_ref, y_ref, sems = scratch
    rows = xa_ref.shape[0] // hidden_ref.shape[1]
    blocks = hidden_ref.shape[0] // rows
    items, width_d = hidden_ref.shape[1:]
    loads = [
        pltpu.make_async_copy(
            hidden_hbm.at[pl.ds(b * rows, rows)], hidden_ref.at[pl.ds(b * rows, rows)], sems.at[b]
        )
        for b in range(blocks)
    ]
    columns = w_hbm.shape[2]
    weights = [
        pltpu.make_async_copy(w_hbm.at[j], w_ref.at[:, pl.ds(j * columns, columns)], sems.at[blocks + j])
        for j in range(3)
    ]
    send = pltpu.make_async_copy(q_ref, q_hbm, sems.at[blocks + 3])
    for load in loads[:1] + weights + loads[1:]:
        load.start()
    trows = text_ref.shape[0]
    total = hidden_ref.shape[0]
    for i in range(items):
        for j in range(2):
            q_ref[i, total + j * trows : total + (j + 1) * trows] = text_ref[:, i, j, :]
    width = w_hbm.shape[2]
    tiles = width // LANES
    gain = gain_ref[...]
    gains = jnp.concatenate(
        [gain[0:1] * 0.125] * (width // HEAD) + [gain[1:2]] * (width // HEAD), axis=1
    )
    shift = mod_ref[0].astype(F32)
    scale = 1.0 + mod_ref[1].astype(F32)
    shift_ref[...] = jnp.concatenate([shift, shift], axis=0)
    scale_ref[...] = jnp.concatenate([scale, scale], axis=0)
    wide = 2 * LANES
    r = lax.broadcasted_iota(jnp.int32, (2 * wide, wide), 0) % wide // HEAD
    c = lax.broadcasted_iota(jnp.int32, (2 * wide, wide), 1) // HEAD
    ones = (r == c).astype(F32).astype(BF)

    def norm_rows(block, x_ref, c):
        first = block * rows + c * 4
        x = hidden_ref[first : first + 4].reshape(16, width_d).astype(F32).reshape(2, 8, width_d)
        center = x - jnp.mean(x, axis=-1, keepdims=True)
        variance = jnp.mean(center * center, axis=-1, keepdims=True)
        normed = center * lax.rsqrt(variance + EPSILON)
        out = normed * scale_ref[...][None] + shift_ref[...][None]
        x_ref[c * 16 : c * 16 + 16, :] = out.reshape(16, width_d).astype(BF)

    def finish_tile(block, n, y):
        if n + wide <= 2 * width:
            high, low = split_bf(y * y)
            square = dot(jnp.concatenate([high, low], axis=1), ones) * (1.0 / HEAD)
            y = y * lax.rsqrt(square + EPSILON) * gains[:, n : n + wide]
        for t in range(y.shape[1] // LANES):
            tile = n // LANES + t
            j = tile // tiles
            y_ref[tile] = y[:, t * LANES : (t + 1) * LANES]
            where = slice(block * rows, (block + 1) * rows)
            to = slice(tile % tiles * LANES, (tile % tiles + 1) * LANES)
            for i in range(items):
                (q_ref, k_ref, v_ref)[j][i, where, to] = y_ref[tile, pl.ds(i, rows, stride=items), :].astype(BF)

    chunks = rows // 4
    pending = []
    for block in range(blocks + 1):
        now, later = (xb_ref, xa_ref) if block % 2 == 0 else (xa_ref, xb_ref)
        if block < blocks:
            loads[block].wait()
        if block == 0:
            for c in range(chunks):
                norm_rows(0, later, c)
            for load in weights:
                load.wait()
            continue
        starts = list(range(0, 3 * width, wide))
        for at, n in enumerate(starts):
            y = dot(now[...], w_ref[:, n : min(n + wide, 3 * width)])
            if block < blocks:
                for c in range(at * chunks // len(starts), (at + 1) * chunks // len(starts)):
                    norm_rows(block, later, c)
            if pending:
                done = pending.pop()
                finish_tile(*done)
                if done[0] == blocks - 1 and done[1] < width <= done[1] + wide:
                    send.start()
            pending.append((block - 1, n, y))
    finish_tile(*pending.pop())
    send.wait()


def project(scalars, hidden, modulation, gains, w, text):
    row_total, items, width_d = hidden.shape
    width = w.shape[2]
    rows = 64
    q_rows = row_total + 2 * text.shape[0]
    vmem = pl.BlockSpec(memory_space=pltpu.VMEM)
    grid_spec = pltpu.PrefetchScalarGridSpec(
        num_scalar_prefetch=1,
        grid=(1,),
        in_specs=[
            pl.BlockSpec(memory_space=pltpu.HBM),
            pl.BlockSpec((None, 3, items, width_d), lambda s, r: (r[4], 0, 0, 0)),
            vmem,
            pl.BlockSpec(memory_space=pltpu.HBM),
            vmem,
        ],
        out_specs=[pl.BlockSpec(memory_space=pltpu.HBM)] + [vmem] * 2,
        scratch_shapes=[
            pltpu.VMEM((items, q_rows, width), BF),
            pltpu.VMEM((row_total, items, width_d), BF),
            pltpu.VMEM((width_d, 3 * width), BF),
            pltpu.VMEM((rows * items, width_d), BF),
            pltpu.VMEM((rows * items, width_d), BF),
            pltpu.VMEM((8, width_d), F32),
            pltpu.VMEM((8, width_d), F32),
            pltpu.VMEM((3 * width // LANES, rows * items, LANES), F32),
            pltpu.SemaphoreType.DMA((row_total // rows + 4,)),
        ],
    )
    return pl.pallas_call(
        project_kernel,
        grid_spec=grid_spec,
        out_shape=[jax.ShapeDtypeStruct((items, q_rows, width), BF)]
        + [jax.ShapeDtypeStruct((items, row_total, width), BF)] * 2,
        compiler_params=params(60),
        cost_estimate=COST,
        name="project",
    )(scalars, hidden, modulation, gains, w, text)


def half_masks():
    lane = lax.broadcasted_iota(jnp.int32, (8, LANES), 1)
    return [(lane < HEAD).astype(F32)[0:1].astype(BF), (lane >= HEAD).astype(F32)[0:1].astype(BF)]


def weigh(values, mask, valid=None):
    ones = jnp.broadcast_to(mask, values.shape)
    both = jnp.concatenate([values * mask, ones], axis=1)
    return both if valid is None else both * valid


def sums_tiles(sums, share):
    count = sums.shape[0] // share
    r = lax.broadcasted_iota(jnp.int32, (share, LANES), 0)
    c = lax.broadcasted_iota(jnp.int32, (share, LANES), 1) % HEAD
    own = (r == c).astype(F32)
    at = lax.broadcasted_iota(jnp.int32, (8, LANES), 0)
    tiles = []
    for u in range(count):
        line = jnp.sum(sums[u * share : (u + 1) * share] * own, axis=0, keepdims=True)
        high = line.astype(BF).astype(F32)
        tiles.append(jnp.where(at == 0, high, jnp.where(at == 1, line - high, 0.0)).astype(BF))
    return tiles


def own_kernel(s_ref, q_ref, k_ref, v_ref, *refs):
    out_refs, part_ref, sems = refs[:PATCHES], refs[PATCHES], refs[PATCHES + 1]
    items, rows, width = k_ref.shape
    share = rows // PATCHES
    masks = half_masks()
    for i in range(items):
        for t in range(width // LANES):
            lanes = slice(t * LANES, (t + 1) * LANES)
            kp, vp, qp = k_ref[i, :, lanes], v_ref[i, :, lanes], q_ref[i, 0:rows, lanes]
            ps = [
                jnp.exp(lax.dot_general(qp * mask, kp, NT, preferred_element_type=F32)).astype(BF)
                for mask in masks
            ]
            acc = dot(
                jnp.concatenate(ps, axis=1), jnp.concatenate([weigh(vp, mask) for mask in masks], axis=0)
            )
            sums = acc[:, LANES:]
            part = (acc[:, :LANES] / sums).astype(BF)
            for u, tile in enumerate(sums_tiles(sums, share)):
                part_ref[u, i, 0:share, lanes] = part[u * share : (u + 1) * share]
                part_ref[u, i, share : share + 8, lanes] = tile
    copies = [
        pltpu.make_async_copy(part_ref.at[s_ref[6] ^ g], out_refs[g], sems.at[g]) for g in range(PATCHES)
    ]
    for copy in copies:
        copy.start()
    for copy in copies:
        copy.wait()


def own_attention(scalars, q, k, v):
    items, rows, width = k.shape
    share = rows // PATCHES
    vmem = pl.BlockSpec(memory_space=pltpu.VMEM)
    return pl.pallas_call(
        own_kernel,
        in_specs=[pl.BlockSpec(memory_space=pltpu.SMEM)] + [vmem] * 3,
        out_specs=[pl.BlockSpec(memory_space=pltpu.HBM)] * PATCHES,
        out_shape=[jax.ShapeDtypeStruct((items, share + 8, width), BF)] * PATCHES,
        scratch_shapes=[
            pltpu.VMEM((PATCHES, items, share + 8, width), BF),
            pltpu.SemaphoreType.DMA((PATCHES,)),
        ],
        compiler_params=params(60),
        cost_estimate=COST,
        name="own",
    )(scalars, q, k, v)


def remote_kernel(s_ref, length_ref, *refs):
    q_all, kv_refs = refs[0], refs[1 : 1 + PATCHES]
    out_ref, text_ref = refs[1 + PATCHES :]
    rows = kv_refs[0].shape[0]
    trows = (q_all.shape[1] - rows) // 2
    share = rows // PATCHES
    group, patch = s_ref[4], s_ref[5]
    q_refs = [q_all.at[lax.rem(patch - o + PATCHES, PATCHES)] for o in range(PATCHES)]
    length = length_ref[patch, group]
    masks = half_masks()
    text_ref[...] = jnp.zeros_like(text_ref)
    good = lax.broadcasted_iota(jnp.int32, (rows, 2 * LANES), 0) < length
    for p in range(PATCHES):
        for j in range(2):
            first = rows + j * trows
            text_ref[j, p * trows : (p + 1) * trows] = q_all[p, first : first + trows].astype(F32)
    valid = good.astype(F32).astype(BF)
    text_k, text_v = text_ref[0].astype(BF), text_ref[1].astype(BF)
    accs = [None] * PATCHES
    for c in range(PATCHES + 1):
        if c == PATCHES:
            keys, values = text_k, [weigh(text_v, mask, valid) for mask in masks]
        else:
            pair = kv_refs[c]
            keys, values = pair[:, 0, :], pair[:, 1, :]
            values = [weigh(values, mask) for mask in masks]
        which = [o for o in range(PATCHES) if o != c]
        queries = jnp.concatenate([q_refs[o][0:rows] for o in which], axis=0)
        ps = [
            jnp.exp(lax.dot_general(queries * mask, keys, NT, preferred_element_type=F32)).astype(BF)
            for mask in masks
        ]
        term = dot(jnp.concatenate(ps, axis=1), jnp.concatenate(values, axis=0))
        for at, o in enumerate(which):
            piece = term[at * rows : (at + 1) * rows]
            accs[o] = piece if accs[o] is None else accs[o] + piece
    for o in range(PATCHES):
        sums = accs[o][:, LANES:]
        part = (accs[o][:, :LANES] / sums).astype(BF)
        base = lax.rem(patch - o + PATCHES, PATCHES) * PATCHES
        for u, tile in enumerate(sums_tiles(sums, share)):
            out_ref[base + u, 0:share] = part[u * share : (u + 1) * share]
            out_ref[base + u, share : share + 8] = tile


def remote_attention(scalars, lengths, q, stale, kvs):
    rows, _, _, width = stale.shape
    q_rows = q.shape[1]
    share = rows // PATCHES
    grid_spec = pltpu.PrefetchScalarGridSpec(
        num_scalar_prefetch=2,
        grid=(width // LANES,),
        in_specs=[pl.BlockSpec((PATCHES, q_rows, LANES), lambda s, r, t: (0, 0, s))]
        + [pl.BlockSpec((rows, None, 2, LANES), lambda s, r, t: (0, r[0], 0, s))]
        + [pl.BlockSpec((rows, 2, LANES), lambda s, r, t: (0, 0, s))] * (PATCHES - 1),
        out_specs=pl.BlockSpec((PATCHES * PATCHES, share + 8, LANES), lambda s, r, t: (0, 0, s)),
        scratch_shapes=[pltpu.VMEM((2, rows, LANES), F32)],
    )
    return pl.pallas_call(
        remote_kernel,
        grid_spec=grid_spec,
        out_shape=jax.ShapeDtypeStruct((PATCHES * PATCHES, share + 8, width), BF),
        compiler_params=params(60),
        cost_estimate=COST,
        name="remote",
    )(scalars, lengths, q, stale, *kvs)


def spread(lines, ones2):
    r = lax.broadcasted_iota(jnp.int32, (HEAD, LANES), 0)
    c = lax.broadcasted_iota(jnp.int32, (HEAD, LANES), 1) % HEAD
    parts = []
    for line in lines:
        f = line.astype(F32)
        parts.append(
            jnp.concatenate(
                [jnp.where(r == c, f[0:1], 0.0), jnp.where(r == c, f[1:2], 0.0)], axis=1
            ).astype(BF)
        )
    return dot(jnp.concatenate(parts, axis=0), ones2)


def finish_kernel(s_ref, far_ref, near0, near1, near2, near3, hidden_hbm, mod_ref, w_own, w1, w2, w3, *refs):
    out_ref, joined_ref, hidden_ref, w0, sems = refs
    nears, ws = [near0, near1, near2, near3], [w0, w1, w2, w3]
    share, items, width_d = hidden_ref.shape
    rows = share * items
    width = w0.shape[0]
    tp = s_ref[6]
    loads = [
        pltpu.make_async_copy(w_own, w0, sems.at[0]),
        pltpu.make_async_copy(
            hidden_hbm.at[pl.ds(pl.multiple_of(tp * share, share), share)], hidden_ref, sems.at[1]
        ),
    ]
    for load in loads:
        load.start()
    ones2 = block_ones(2 * LANES)
    a = lax.broadcasted_iota(jnp.int32, (rows, rows), 0)
    b = lax.broadcasted_iota(jnp.int32, (rows, rows), 1)
    order = ((a % items) * share + a // items == b).astype(F32).astype(BF)
    for g in range(4):
        source = tp ^ g
        mixed = []
        for t in range(width // LANES):
            lanes = slice(t * LANES, (t + 1) * LANES)
            parts = [far_ref[i, source, :, lanes] for i in range(items)]
            parts += [nears[g][i, :, lanes] for i in range(items)]
            sums = spread([x[share:] for x in parts], ones2)
            values = jnp.concatenate([x[:share] for x in parts], axis=0).astype(F32)
            total = values[:rows] * sums[:rows] + values[rows:] * sums[rows:]
            mixed.append((total / (sums[:rows] + sums[rows:])).astype(BF))
        joined_ref[g] = dot(order, jnp.concatenate(mixed, axis=1)).astype(BF)
    for load in loads:
        load.wait()
    gate = mod_ref[2].astype(F32)
    gate = jnp.concatenate([gate, gate], axis=0)[None]
    for n in range(0, width_d, 256):
        lanes = slice(n, min(n + 256, width_d))
        acc = None
        for g in range(4):
            term = dot(joined_ref[g], ws[g][:, lanes]).astype(BF).astype(F32)
            acc = term if acc is None else acc + term
        size = lanes.stop - n
        own = hidden_ref[:, :, lanes].reshape(rows, size).astype(F32).reshape(rows // 8, 8, size)
        new = own + gate[:, :, lanes] * acc.reshape(rows // 8, 8, size)
        out_ref[:, :, lanes] = new.reshape(rows, size).astype(BF).reshape(share, items, size)


def finish(scalars, far, near, hidden, modulation, ws):
    row_total, items, width_d = hidden.shape
    share = row_total // PATCHES
    width = ws[0].shape[0]
    vmem = pl.BlockSpec(memory_space=pltpu.VMEM)
    hbm = pl.BlockSpec(memory_space=pltpu.HBM)
    grid_spec = pltpu.PrefetchScalarGridSpec(
        num_scalar_prefetch=1,
        grid=(1,),
        in_specs=[pl.BlockSpec((items, 4, share + 8, width), lambda s, r: (0, 0, 0, 0))]
        + [vmem] * 4
        + [hbm, pl.BlockSpec((None, 3, items, width_d), lambda s, r: (r[4], 0, 0, 0)), hbm]
        + [vmem] * 3,
        out_specs=pl.BlockSpec((share, items, width_d), lambda s, r: (0, 0, 0)),
        scratch_shapes=[
            pltpu.VMEM((4, share * items, width), BF),
            pltpu.VMEM((share, items, width_d), BF),
            pltpu.VMEM((width, width_d), BF),
            pltpu.SemaphoreType.DMA((2,)),
        ],
    )
    return pl.pallas_call(
        finish_kernel,
        grid_spec=grid_spec,
        out_shape=jax.ShapeDtypeStruct((share, items, width_d), BF),
        compiler_params=params(60),
        cost_estimate=COST,
        name="finish",
    )(scalars, far, *near, hidden, modulation, *ws)


def body(layout, hidden, modulation, w_qkv, w_out, qk_gain, stale_kv, text_kv, text_len):
    slots, tps, groups, w_pairs, core_pairs = layout
    place = lax.axis_index("req")
    tp = lax.axis_index("tp")
    group = place % groups
    patch = place // groups
    items_at = [(patch + o) % PATCHES for o in range(PATCHES)]
    scalars = jnp.stack([v.astype(jnp.int32) for v in items_at + [group, patch, tp]])
    both = ("req", "tp")

    columns = [[g + groups * p for p in range(PATCHES)] for g in range(groups)]
    rings = [[place * tps + t for place in column for t in range(tps)] for column in columns]

    def along_x(value, by):
        return lax.ppermute(value, "req", [(i, (i + by * groups) % slots) for i in range(slots)])

    raws = [lax.dynamic_index_in_dim(stale_kv[0], items_at[o], 1, keepdims=False) for o in range(1, PATCHES)]
    raws, scalars, w_own = lax.optimization_barrier((raws, scalars, w_out))
    kvs = [along_x(raws[o - 1], o) for o in range(1, PATCHES)]
    w_far = lax.ppermute(w_own, both, w_pairs)
    w_near = lax.ppermute(w_own, both, core_pairs)
    mod = jnp.transpose(modulation, (0, 2, 1, 3))
    q, k, v = project(scalars, hidden[0], mod, qk_gain, jnp.transpose(w_qkv, (1, 0, 2)), text_kv[0])
    q_sent, kvs = lax.optimization_barrier((q, kvs))
    q_all = lax.all_to_all(q_sent, "req", 0, 0, axis_index_groups=columns, tiled=True)
    w_across = lax.ppermute(w_far, both, core_pairs)
    owns = own_attention(scalars, q, k, v)
    near = [owns[0]] + [
        lax.ppermute(owns[g], "tp", [(i, i ^ g) for i in range(tps)]) for g in range(1, tps)
    ]
    sent = remote_attention(scalars, jnp.transpose(text_len), q_all, stale_kv[0], kvs)
    sent, near = lax.optimization_barrier((sent, near))
    far = lax.all_to_all(sent, both, 0, 0, axis_index_groups=rings, tiled=True)
    far = far.reshape(PATCHES, tps, *far.shape[1:])
    fresh = jnp.transpose(jnp.stack([k, v], axis=0), (2, 1, 0, 3))
    updated = finish(scalars, far, near, hidden[0], mod, [w_out, w_near, w_far, w_across])
    return (updated[None], fresh[None])


def solution(mesh):
    slots, tps = mesh.shape["req"], mesh.shape["tp"]
    groups = slots // PATCHES
    ring = 8
    w_pairs = []
    for place in range(slots):
        column, high = place // (ring // 2), place % (ring // 2)
        for t in range(tps):
            low, core = t // 2, t % 2
            z = 2 * high + low
            z = (z + (1 if low else -1)) % ring if core else z ^ 1
            target = column * (ring // 2) + z // 2
            w_pairs.append((place * tps + t, target * tps + z % 2 * 2 + core))
    core_pairs = [(i, i ^ 1) for i in range(slots * tps)]
    layout = (slots, tps, groups, w_pairs, core_pairs)
    return jax.shard_map(
        functools.partial(body, layout),
        mesh=mesh,
        in_specs=(
            P("req", None, None, None),
            P(),
            P(None, None, "tp"),
            P("tp", None),
            P(),
            P("req", None, None, None, "tp"),
            P("req", None, None, None, "tp"),
            P(),
        ),
        out_specs=(P("req", "tp", None, None), P("req", None, None, None, "tp")),
        check_vma=False,
    )
```

time: 114 us -> 89.4 us (0.78)
  Pallas kernels: 54.7 us -> 42.9 us
  waiting for transfers between devices: 25.4 us -> 15.7 us
  starting transfers between devices: 23.5 us -> 21.6 us
  local copies, waits for them, and re-layouts: 9.13 us -> 7.37 us
    ppermute x3, waiting for transfers between devices: 16.4 us -> 0.01 us  [body(): lax.ppermute(owns[g], 'tp', [(i, i ^ g) for i in range(tps)])]
    pallas_call x5 -> x1, Pallas kernels: 17.5 us -> 4.65 us  [own_attention(): pl.pallas_call(own_kernel, in_specs=[pl.BlockSpec(memory_space=pltpu.SMEM...]
    all_to_all x1, waiting for transfers between devices: 0.01 us -> 9.82 us  [body(): far = lax.all_to_all(sent, both, 0, 0, axis_index_groups=rings, tiled=True)]
    ppermute x6 -> x3, waiting for transfers between devices: 8.95 us -> 0.01 us  [along_x(): lax.ppermute(value, 'req', [(i, (i + by * groups) % slots) for i in range...]
    all_to_all x0 -> x1, waiting for transfers between devices: none -> 5.85 us  [body(): lax.all_to_all(q_sent, 'req', 0, 0, axis_index_groups=columns, tiled=True)]
    all_to_all x0 -> x1, starting transfers between devices: none -> 3.75 us  [body(): lax.all_to_all(q_sent, 'req', 0, 0, axis_index_groups=columns, tiled=True)]
    ppermute x6 -> x3, starting transfers between devices: 7.92 us -> 4.82 us  [along_x(): lax.ppermute(value, 'req', [(i, (i + by * groups) % slots) for i in range...]
    ppermute x2, starting transfers between devices: 8.28 us -> 6.41 us  [the longest x1 6.41 us: body(): w_far = lax.ppermute(w_own, both, w_pairs)]
  transfers between devices with their start and end apart: 13 -> 11, of which waited for: 4 -> 2; matrix products, arithmetic and copies ran while one was open for 6% -> 3% of each run, Pallas kernels for 39% -> 37%
where the time goes in v2:
time: 89.4 us; the launch traced here: 89 us
  Pallas kernels  42.9 us (48%)
  starting transfers between devices  21.6 us (24%)
  waiting for transfers between devices  15.7 us (18%)
  local copies, waits for them, and re-layouts  7.37 us (8%)
  between operations  1.16 us (1%)
    pallas_call x1, Pallas kernels, project(): pl.pallas_call(project_kernel, grid_spec=grid_spec, out_shape=[jax.ShapeD...  17.1 us
    pallas_call x1, Pallas kernels, remote_attention(): pl.pallas_call(remote_kernel, grid_spec=grid_spec, out_shape=jax.ShapeDty...  11.5 us
    all_to_all x1, waiting for transfers between devices, body(): far = lax.all_to_all(sent, both, 0, 0, axis_index_groups=rings, tiled=True)  9.82 us
    pallas_call x1, Pallas kernels, finish(): pl.pallas_call(finish_kernel, grid_spec=grid_spec, out_shape=jax.ShapeDty...  9.72 us
    ppermute x1, starting transfers between devices, body(): w_far = lax.ppermute(w_own, both, w_pairs)  6.41 us
    all_to_all x1, waiting for transfers between devices, body(): lax.all_to_all(q_sent, 'req', 0, 0, axis_index_groups=columns, tiled=True)  5.85 us
    ppermute x3, starting transfers between devices, along_x(): lax.ppermute(value, 'req', [(i, (i + by * groups) % slots) for i in range...  4.82 us
    unnamed x21, local copies, waits for them, and re-layouts  4.68 us
  transfers between devices with their start and end apart: 11, of which 2 were waited for; matrix products, arithmetic and copies ran while one was open for 3% of the time, Pallas kernels for 37%

profile of v2, /device:TPU:1, one launch (start us, length us, event | category | flops | bytes accessed | tf_op | source)
XLA Modules:
  0.0 89.0 jit_solution(810746198623416421)
XLA Ops:
  0.7 2.1 %dynamic-slice_bitcast_fusion = (bf16[256,2,384]{2,1,0:T(2,128)(2,1)S(1)}, bf16[256,2,384]{2,1,0:T(2,128)(2,1)S(1)}, bf16[256,2,384]{2,1,0:T(2,128)(2,1)S(1)}) fusion(bf16[1,256,4,2,384]{4,3,2,1,0:T(2,128)(2,1)} %param.13, s32[]{:T(128)S(6)} %select_n.43, s32[]{:T(128)S(6)} %select_n.41, s32[]{:T(128)S(6)} %select_n.39), kind=kLoop, calls=%fused_computation.1 | loop fusion | bytes 2359308 | tf_op jit(solution)/shard_map/jit(dynamic_index_in_dim)/squeeze | solution.py:419
  2.8 0.6 stack.40.s_ref
  3.4 6.4 %collective-permute-start.7 = (bf16[384,2432]{1,0:T(8,128)(2,1)}, bf16[384,2432]{1,0:T(8,128)(2,1)}, u32[]{:S(2)}, u32[]{:S(2)}) collective-permute-start(bf16[384,2432]{1,0:T(8,128)(2,1)} %w_own.1), channel_id=1, source_target_pairs={{0,2},{1,15},{2,0},{3,5},{4,6},{5,3},{6,4},{7,9},{8,10},{9,7},{10,... | collective-permute-start | bytes 5603336 | tf_op jit(solution)/shard_map/ppermute | solution.py:422
  9.8 1.2 %collective-permute-start = (bf16[256,2,384]{2,1,0:T(2,128)(2,1)S(1)}, bf16[256,2,384]{2,1,0:T(2,128)(2,1)S(1)}, u32[]{:S(2)}, u32[]{:S(2)}) collective-permute-start(bf16[256,2,384]{2,1,0:T(2,128)(2,1)S(1)} %get-tuple-element.25), channel_id=1, source_target_pairs={{0,64},{4,68},{8,72},{12,76},{16,80},{20,84},{24,88},{28,92},{32,9... | collective-permute-start | bytes 1179656 | tf_op jit(solution)/shard_map/ppermute | solution.py:417
  11.0 2.5 %collective-permute-start.1 = (bf16[256,2,384]{2,1,0:T(2,128)(2,1)S(1)}, bf16[256,2,384]{2,1,0:T(2,128)(2,1)S(1)}, u32[]{:S(2)}, u32[]{:S(2)}) collective-permute-start(bf16[256,2,384]{2,1,0:T(2,128)(2,1)S(1)} %get-tuple-element.26), channel_id=1, source_target_pairs={{0,128},{4,132},{8,136},{12,140},{16,144},{20,148},{24,152},{28,15... | collective-permute-start | bytes 1179656 | tf_op jit(solution)/shard_map/ppermute | solution.py:417
  13.5 1.2 %collective-permute-start.2 = (bf16[256,2,384]{2,1,0:T(2,128)(2,1)S(1)}, bf16[256,2,384]{2,1,0:T(2,128)(2,1)S(1)}, u32[]{:S(2)}, u32[]{:S(2)}) collective-permute-start(bf16[256,2,384]{2,1,0:T(2,128)(2,1)S(1)} %get-tuple-element.27), channel_id=1, source_target_pairs={{0,192},{4,196},{8,200},{12,204},{16,208},{20,212},{24,216},{28,22... | collective-permute-start | bytes 1179656 | tf_op jit(solution)/shard_map/ppermute | solution.py:417
  14.7 17.1 %project.1 = (bf16[4,336,384]{2,1,0:T(8,128)(2,1)}, bf16[4,256,384]{2,1,0:T(8,128)(2,1)}, bf16[4,256,384]{2,1,0:T(8,128)(2,1)}) custom-call(s32[7]{0:T(128)} %stack.40.s_ref, bf16[256,4,2432]{2,1,0:T(4,128)(2,1)} %bitcast.27, bf16[16,3,4,2432]{3,2,1,0:T(4,128)(2,1)} %bitcast.31, f32[2,64]{1,0:T(2,128)} %gain_ref.1, bf16[3,2432,384]{2,1,0:T(8,128)(2,1)} %bitcast.29, ...), custom_call_target="tpu_custom_call" | custom-call | flops 1000 | bytes 1000 | tf_op jit(solution)/shard_map/project/pallas_call | solution.py:158
  31.7 0.0 collective-permute-done.refs_2_
  31.7 0.0 collective-permute-done.1.refs_3_
  31.8 0.0 collective-permute-done.2.refs_4_
  31.8 3.7 %all-to-all-start = ((bf16[4,336,384]{2,1,0:T(8,128)(2,1)}), bf16[4,336,384]{2,1,0:T(8,128)(2,1)S(1)}, u32[]{:S(2)}, u32[]{:S(2)}) async-start(bf16[4,336,384]{2,1,0:T(8,128)(2,1)} %get-tuple-element.28.q_ref), calls=%async_computation | async-start | bytes 2064384 | tf_op jit(solution)/shard_map/all_to_all | solution.py:427
  35.5 4.6 %own.1 = (bf16[4,72,384]{2,1,0:T(8,128)(2,1)}, bf16[4,72,384]{2,1,0:T(8,128)(2,1)}, bf16[4,72,384]{2,1,0:T(8,128)(2,1)}, bf16[4,72,384]{2,1,0:T(8,128)(2,1)}) custom-call(s32[7]{0:T(128)} %stack.40.s_ref, bf16[4,336,384]{2,1,0:T(8,128)(2,1)} %get-tuple-element.28.q_ref, bf16[4,256,384]{2,1,0:T(8,128)(2,1)} %get-tuple-element.32.k_ref, ...), custom_call_target="tpu_custom_call" | custom-call | flops 1000 | bytes 1000 | tf_op jit(solution)/shard_map/own/pallas_call | solution.py:228
  40.2 0.1 collective-permute-start.3
  40.3 0.1 collective-permute-start.4
  40.4 2.0 %collective-permute-start.5 = (bf16[4,72,384]{2,1,0:T(8,128)(2,1)}, bf16[4,72,384]{2,1,0:T(8,128)(2,1)S(1)}, u32[]{:S(2)}, u32[]{:S(2)}) collective-permute-start(bf16[4,72,384]{2,1,0:T(8,128)(2,1)} %get-tuple-element.37), channel_id=1, source_target_pairs={{0,3},{1,2},{2,1},{3,0},{4,7},{5,6},{6,5},{7,4},{8,11},{9,10},{10,... | collective-permute-start | bytes 663560 | tf_op jit(solution)/shard_map/ppermute | solution.py:431
  42.5 0.0 collective-permute-start.6
  42.5 0.0 collective-permute-done.7.w2
  42.5 0.5 collective-permute-start.8
  43.0 5.9 %all-to-all-done.refs_0_ = bf16[4,336,384]{2,1,0:T(8,128)(2,1)S(1)} async-done(((bf16[4,336,384]{2,1,0:T(8,128)(2,1)}), bf16[4,336,384]{2,1,0:T(8,128)(2,1)S(1)}, u32[]{:S(2)}, u32[]{:S(2)}) %all-to-all-start) | async-done | bytes 1032224 | tf_op jit(solution)/shard_map/all_to_all | solution.py:427
  48.8 1.0 %copy-done = bf16[4,336,384]{2,1,0:T(8,128)(2,1)} copy-done((bf16[4,336,384]{2,1,0:T(8,128)(2,1)}, bf16[4,336,384]{2,1,0:T(8,128)(2,1)S(1)}, u32[]{:S(2)}) %copy-start) | copy-done | bytes 1032216
  49.8 11.5 %remote.1 = bf16[16,72,384]{2,1,0:T(8,128)(2,1)} custom-call(s32[7]{0:T(128)} %stack.40.s_ref, s32[4,16]{1,0:T(4,128)} %bitcast.38, bf16[4,336,384]{2,1,0:T(8,128)(2,1)} %copy-done, bf16[256,4,2,384]{3,2,1,0:T(2,128)(2,1)} %bitcast.30, bf16[256,2,384]{2,1,0:T(2,128)(2,1)} %copy-done.4, bf16[256,2,384]{2,1,0:T(2,128)(2,1)} %copy-done.5, ...), custom_call_target="tpu_custom_call" | custom-call | flops 1000 | bytes 1000 | tf_op jit(solution)/shard_map/remote/pallas_call | solution.py:301
  61.3 0.0 collective-permute-done.3.near1
  61.3 0.0 collective-permute-done.4.near2
  61.3 0.0 collective-permute-done.5.near3
  61.4 3.9 %all-to-all-start.1 = ((bf16[16,72,384]{2,1,0:T(8,128)(2,1)}), bf16[16,72,384]{2,1,0:T(8,128)(2,1)S(1)}, u32[]{:S(2)}, u32[]{:S(2)}) async-start(bf16[16,72,384]{2,1,0:T(8,128)(2,1)} %remote.1), calls=%async_computation.1 | async-start | bytes 1769472 | tf_op jit(solution)/shard_map/all_to_all | solution.py:435
  65.3 0.2 maximum_bitcast_fusion
  65.5 2.8 %copy.10 = bf16[1,256,4,2,384]{4,3,2,1,0:T(2,128)(2,1)} copy(bf16[1,256,4,2,384]{4,1,2,3,0:T(8,128)(2,1)S(1)} %maximum_bitcast_fusion) | data formatting | bytes 3145728
  68.3 0.0 collective-permute-done.6.w1
  68.3 9.8 %all-to-all-done.1 = bf16[16,72,384]{2,1,0:T(8,128)(2,1)S(1)} async-done(((bf16[16,72,384]{2,1,0:T(8,128)(2,1)}), bf16[16,72,384]{2,1,0:T(8,128)(2,1)S(1)}, u32[]{:S(2)}, u32[]{:S(2)}) %all-to-all-start.1) | async-done | bytes 884768 | tf_op jit(solution)/shard_map/all_to_all | solution.py:435
  78.1 0.0 collective-permute-done.8.w3
  78.1 0.9 %copy-done.1 = bf16[16,72,384]{2,1,0:T(8,128)(2,1)} copy-done((bf16[16,72,384]{2,1,0:T(8,128)(2,1)}, bf16[16,72,384]{2,1,0:T(8,128)(2,1)S(1)}, u32[]{:S(2)}) %copy-start.1) | copy-done | bytes 884760
  79.0 9.7 %finish.1 = bf16[64,4,2432]{2,1,0:T(4,128)(2,1)} custom-call(s32[7]{0:T(128)} %stack.40.s_ref, bf16[4,4,72,384]{3,2,1,0:T(8,128)(2,1)} %bitcast.33, bf16[4,72,384]{2,1,0:T(8,128)(2,1)} %get-tuple-element.39.near0, bf16[4,72,384]{2,1,0:T(8,128)(2,1)} %copy-done.7, bf16[4,72,384]{2,1,0:T(8,128)(2,1)} %copy-done.8, bf16[4,72,384]{2,1,0:T(8,128)(2,1)} %copy-done.9, ...), custom_call_target="tpu_custom_call" | custom-call | flops 1000 | bytes 1000 | tf_op jit(solution)/shard_map/finish/pallas_call | solution.py:393
  (18 shorter events, 0.0 us)
Async XLA Ops:
  3.4 39.0 %collective-permute-start.7 = (bf16[384,2432]{1,0:T(8,128)(2,1)}, bf16[384,2432]{1,0:T(8,128)(2,1)}, u32[]{:S(2)}, u32[]{:S(2)}) collective-permute-start(bf16[384,2432]{1,0:T(8,128)(2,1)} %w_own.1), channel_id=1, source_target_pairs={{0,2},{1,15},{2,0},{3,5},{4,6},{5,3},{6,4},{7,9},{8,10},{9,7},{10,... | collective-permute-start | bytes 5603336 | tf_op jit(solution)/shard_map/ppermute | solution.py:422
  9.8 21.9 %collective-permute-start = (bf16[256,2,384]{2,1,0:T(2,128)(2,1)S(1)}, bf16[256,2,384]{2,1,0:T(2,128)(2,1)S(1)}, u32[]{:S(2)}, u32[]{:S(2)}) collective-permute-start(bf16[256,2,384]{2,1,0:T(2,128)(2,1)S(1)} %get-tuple-element.25), channel_id=1, source_target_pairs={{0,64},{4,68},{8,72},{12,76},{16,80},{20,84},{24,88},{28,92},{32,9... | collective-permute-start | bytes 1179656 | tf_op jit(solution)/shard_map/ppermute | solution.py:417
  11.0 20.7 %collective-permute-start.1 = (bf16[256,2,384]{2,1,0:T(2,128)(2,1)S(1)}, bf16[256,2,384]{2,1,0:T(2,128)(2,1)S(1)}, u32[]{:S(2)}, u32[]{:S(2)}) collective-permute-start(bf16[256,2,384]{2,1,0:T(2,128)(2,1)S(1)} %get-tuple-element.26), channel_id=1, source_target_pairs={{0,128},{4,132},{8,136},{12,140},{16,144},{20,148},{24,152},{28,15... | collective-permute-start | bytes 1179656 | tf_op jit(solution)/shard_map/ppermute | solution.py:417
  13.5 18.3 %collective-permute-start.2 = (bf16[256,2,384]{2,1,0:T(2,128)(2,1)S(1)}, bf16[256,2,384]{2,1,0:T(2,128)(2,1)S(1)}, u32[]{:S(2)}, u32[]{:S(2)}) collective-permute-start(bf16[256,2,384]{2,1,0:T(2,128)(2,1)S(1)} %get-tuple-element.27), channel_id=1, source_target_pairs={{0,192},{4,196},{8,200},{12,204},{16,208},{20,212},{24,216},{28,22... | collective-permute-start | bytes 1179656 | tf_op jit(solution)/shard_map/ppermute | solution.py:417
  31.7 8.5 %copy-start.4 = (bf16[256,2,384]{2,1,0:T(2,128)(2,1)}, bf16[256,2,384]{2,1,0:T(2,128)(2,1)S(1)}, u32[]{:S(2)}) copy-start(bf16[256,2,384]{2,1,0:T(2,128)(2,1)S(1)} %collective-permute-done.refs_2_) | copy-start | bytes 1179652
  31.8 8.5 %copy-start.5 = (bf16[256,2,384]{2,1,0:T(2,128)(2,1)}, bf16[256,2,384]{2,1,0:T(2,128)(2,1)S(1)}, u32[]{:S(2)}) copy-start(bf16[256,2,384]{2,1,0:T(2,128)(2,1)S(1)} %collective-permute-done.1.refs_3_) | copy-start | bytes 1179652
  31.8 8.4 %copy-start.6 = (bf16[256,2,384]{2,1,0:T(2,128)(2,1)}, bf16[256,2,384]{2,1,0:T(2,128)(2,1)S(1)}, u32[]{:S(2)}) copy-start(bf16[256,2,384]{2,1,0:T(2,128)(2,1)S(1)} %collective-permute-done.2.refs_4_) | copy-start | bytes 1179652
  31.8 17.0 %all-to-all-start = ((bf16[4,336,384]{2,1,0:T(8,128)(2,1)}), bf16[4,336,384]{2,1,0:T(8,128)(2,1)S(1)}, u32[]{:S(2)}, u32[]{:S(2)}) async-start(bf16[4,336,384]{2,1,0:T(8,128)(2,1)} %get-tuple-element.28.q_ref), calls=%async_computation | async-start | bytes 2064384 | tf_op jit(solution)/shard_map/all_to_all | solution.py:427
  40.2 21.1 %collective-permute-start.3 = (bf16[4,72,384]{2,1,0:T(8,128)(2,1)}, bf16[4,72,384]{2,1,0:T(8,128)(2,1)S(1)}, u32[]{:S(2)}, u32[]{:S(2)}) collective-permute-start(bf16[4,72,384]{2,1,0:T(8,128)(2,1)} %get-tuple-element.35), channel_id=1, source_target_pairs={{0,1},{1,0},{2,3},{3,2},{4,5},{5,4},{6,7},{7,6},{8,9},{9,8},{10,11... | collective-permute-start | bytes 663560 | tf_op jit(solution)/shard_map/ppermute | solution.py:431
  40.3 21.0 %collective-permute-start.4 = (bf16[4,72,384]{2,1,0:T(8,128)(2,1)}, bf16[4,72,384]{2,1,0:T(8,128)(2,1)S(1)}, u32[]{:S(2)}, u32[]{:S(2)}) collective-permute-start(bf16[4,72,384]{2,1,0:T(8,128)(2,1)} %get-tuple-element.36), channel_id=1, source_target_pairs={{0,2},{1,3},{2,0},{3,1},{4,6},{5,7},{6,4},{7,5},{8,10},{9,11},{10,... | collective-permute-start | bytes 663560 | tf_op jit(solution)/shard_map/ppermute | solution.py:431
  40.4 20.9 %collective-permute-start.5 = (bf16[4,72,384]{2,1,0:T(8,128)(2,1)}, bf16[4,72,384]{2,1,0:T(8,128)(2,1)S(1)}, u32[]{:S(2)}, u32[]{:S(2)}) collective-permute-start(bf16[4,72,384]{2,1,0:T(8,128)(2,1)} %get-tuple-element.37), channel_id=1, source_target_pairs={{0,3},{1,2},{2,1},{3,0},{4,7},{5,6},{6,5},{7,4},{8,11},{9,10},{10,... | collective-permute-start | bytes 663560 | tf_op jit(solution)/shard_map/ppermute | solution.py:431
  42.5 25.8 %collective-permute-start.6 = (bf16[384,2432]{1,0:T(8,128)(2,1)}, bf16[384,2432]{1,0:T(8,128)(2,1)}, u32[]{:S(2)}, u32[]{:S(2)}) collective-permute-start(bf16[384,2432]{1,0:T(8,128)(2,1)} %w_own.1), channel_id=1, source_target_pairs={{0,1},{1,0},{2,3},{3,2},{4,5},{5,4},{6,7},{7,6},{8,9},{9,8},{10,11... | collective-permute-start | bytes 5603336 | tf_op jit(solution)/shard_map/ppermute | solution.py:423
  42.5 35.6 %collective-permute-start.8 = (bf16[384,2432]{1,0:T(8,128)(2,1)}, bf16[384,2432]{1,0:T(8,128)(2,1)}, u32[]{:S(2)}, u32[]{:S(2)}) collective-permute-start(bf16[384,2432]{1,0:T(8,128)(2,1)} %collective-permute-done.7.w2), channel_id=1, source_target_pairs={{0,1},{1,0},{2,3},{3,2},{4,5},{5,4},{6,7},{7,6},{8,9},{9,8},{10,11... | collective-permute-start | bytes 5603336 | tf_op jit(solution)/shard_map/ppermute | solution.py:428
  48.8 1.0 %copy-start = (bf16[4,336,384]{2,1,0:T(8,128)(2,1)}, bf16[4,336,384]{2,1,0:T(8,128)(2,1)S(1)}, u32[]{:S(2)}) copy-start(bf16[4,336,384]{2,1,0:T(8,128)(2,1)S(1)} %all-to-all-done.refs_0_) | copy-start | bytes 3096580
  61.3 4.0 %copy-start.2 = (bf16[4,256,384]{2,1,0:T(8,128)(2,1)S(1)}, bf16[4,256,384]{2,1,0:T(8,128)(2,1)}, u32[]{:S(2)}) copy-start(bf16[4,256,384]{2,1,0:T(8,128)(2,1)} %get-tuple-element.32.k_ref) | copy-start | bytes 2359300
  61.3 4.0 %copy-start.3 = (bf16[4,256,384]{2,1,0:T(8,128)(2,1)S(1)}, bf16[4,256,384]{2,1,0:T(8,128)(2,1)}, u32[]{:S(2)}) copy-start(bf16[4,256,384]{2,1,0:T(8,128)(2,1)} %get-tuple-element.33.v_ref) | copy-start | bytes 2359300
  61.3 4.2 %copy-start.7 = (bf16[4,72,384]{2,1,0:T(8,128)(2,1)}, bf16[4,72,384]{2,1,0:T(8,128)(2,1)S(1)}, u32[]{:S(2)}) copy-start(bf16[4,72,384]{2,1,0:T(8,128)(2,1)S(1)} %collective-permute-done.3.near1) | copy-start | bytes 663556
  61.3 4.2 %copy-start.8 = (bf16[4,72,384]{2,1,0:T(8,128)(2,1)}, bf16[4,72,384]{2,1,0:T(8,128)(2,1)S(1)}, u32[]{:S(2)}) copy-start(bf16[4,72,384]{2,1,0:T(8,128)(2,1)S(1)} %collective-permute-done.4.near2) | copy-start | bytes 663556
  61.3 4.2 %copy-start.9 = (bf16[4,72,384]{2,1,0:T(8,128)(2,1)}, bf16[4,72,384]{2,1,0:T(8,128)(2,1)S(1)}, u32[]{:S(2)}) copy-start(bf16[4,72,384]{2,1,0:T(8,128)(2,1)S(1)} %collective-permute-done.5.near3) | copy-start | bytes 663556
  61.4 16.8 %all-to-all-start.1 = ((bf16[16,72,384]{2,1,0:T(8,128)(2,1)}), bf16[16,72,384]{2,1,0:T(8,128)(2,1)S(1)}, u32[]{:S(2)}, u32[]{:S(2)}) async-start(bf16[16,72,384]{2,1,0:T(8,128)(2,1)} %remote.1), calls=%async_computation.1 | async-start | bytes 1769472 | tf_op jit(solution)/shard_map/all_to_all | solution.py:435
  78.1 0.9 %copy-start.1 = (bf16[16,72,384]{2,1,0:T(8,128)(2,1)}, bf16[16,72,384]{2,1,0:T(8,128)(2,1)S(1)}, u32[]{:S(2)}) copy-start(bf16[16,72,384]{2,1,0:T(8,128)(2,1)S(1)} %all-to-all-done.1) | copy-start | bytes 2654212

commit v3 on v2

--- a/solution.py
+++ b/solution.py
@@ -129,7 +129,7 @@
 def project(scalars, hidden, modulation, gains, w, text):
     row_total, items, width_d = hidden.shape
     width = w.shape[2]
-    rows = 64
+    rows = 128
     q_rows = row_total + 2 * text.shape[0]
     vmem = pl.BlockSpec(memory_space=pltpu.VMEM)
     grid_spec = pltpu.PrefetchScalarGridSpec(
@@ -302,7 +302,7 @@
         remote_kernel,
         grid_spec=grid_spec,
         out_shape=jax.ShapeDtypeStruct((PATCHES * PATCHES, share + 8, width), BF),
-        compiler_params=params(60),
+        compiler_params=params(63),
         cost_estimate=COST,
         name="remote",
     )(scalars, lengths, q, stale, *kvs)

time: 89.4 us -> 88.8 us (level)
  local copies, waits for them, and re-layouts: 7.37 us -> 6.45 us
  Pallas kernels: 42.9 us -> 42 us
    unnamed x21 -> x17, local copies, waits for them, and re-layouts: 4.68 us -> 3.72 us
where the time goes in v3:
time: 88.8 us; the launch traced here: 88.3 us
  Pallas kernels  42 us (47%)
  starting transfers between devices  22.4 us (25%)
  waiting for transfers between devices  16.1 us (18%)
  local copies, waits for them, and re-layouts  6.45 us (7%)
  between operations  1.15 us (1%)
    pallas_call x1, Pallas kernels, project(): pl.pallas_call(project_kernel, grid_spec=grid_spec, out_shape=[jax.ShapeD...  16.2 us
    pallas_call x1, Pallas kernels, remote_attention(): pl.pallas_call(remote_kernel, grid_spec=grid_spec, out_shape=jax.ShapeDty...  11.4 us
    all_to_all x1, waiting for transfers between devices, body(): far = lax.all_to_all(sent, both, 0, 0, axis_index_groups=rings, tiled=True)  9.93 us
    pallas_call x1, Pallas kernels, finish(): pl.pallas_call(finish_kernel, grid_spec=grid_spec, out_shape=jax.ShapeDty...  9.72 us
    ppermute x1, starting transfers between devices, body(): w_far = lax.ppermute(w_own, both, w_pairs)  6.41 us
    all_to_all x1, waiting for transfers between devices, body(): lax.all_to_all(q_sent, 'req', 0, 0, axis_index_groups=columns, tiled=True)  6.18 us
    ppermute x3, starting transfers between devices, along_x(): lax.ppermute(value, 'req', [(i, (i + by * groups) % slots) for i in range...  4.82 us
    pallas_call x1, Pallas kernels, own_attention(): pl.pallas_call(own_kernel, in_specs=[pl.BlockSpec(memory_space=pltpu.SMEM...  4.63 us
  transfers between devices with their start and end apart: 11, of which 2 were waited for; matrix products, arithmetic and copies ran while one was open for 3% of the time, Pallas kernels for 37%

profile of v3, /device:TPU:1, one launch (start us, length us, event | category | flops | bytes accessed | tf_op | source)
XLA Modules:
  0.0 88.3 jit_solution(2214753919586270131)
XLA Ops:
  0.7 2.1 %dynamic-slice_bitcast_fusion = (bf16[256,2,384]{2,1,0:T(2,128)(2,1)S(1)}, bf16[256,2,384]{2,1,0:T(2,128)(2,1)S(1)}, bf16[256,2,384]{2,1,0:T(2,128)(2,1)S(1)}) fusion(bf16[1,256,4,2,384]{4,3,2,1,0:T(2,128)(2,1)} %param.13, s32[]{:T(128)S(6)} %select_n.43, s32[]{:T(128)S(6)} %select_n.41, s32[]{:T(128)S(6)} %select_n.39), kind=kLoop, calls=%fused_computation.1 | loop fusion | bytes 2359308 | tf_op jit(solution)/shard_map/jit(dynamic_index_in_dim)/squeeze | solution.py:419
  2.8 0.7 stack.40.s_ref
  3.5 6.4 %collective-permute-start.7 = (bf16[384,2432]{1,0:T(8,128)(2,1)}, bf16[384,2432]{1,0:T(8,128)(2,1)}, u32[]{:S(2)}, u32[]{:S(2)}) collective-permute-start(bf16[384,2432]{1,0:T(8,128)(2,1)} %w_own.1), channel_id=1, source_target_pairs={{0,2},{1,15},{2,0},{3,5},{4,6},{5,3},{6,4},{7,9},{8,10},{9,7},{10,... | collective-permute-start | bytes 5603336 | tf_op jit(solution)/shard_map/ppermute | solution.py:422
  9.9 1.2 %collective-permute-start = (bf16[256,2,384]{2,1,0:T(2,128)(2,1)S(1)}, bf16[256,2,384]{2,1,0:T(2,128)(2,1)S(1)}, u32[]{:S(2)}, u32[]{:S(2)}) collective-permute-start(bf16[256,2,384]{2,1,0:T(2,128)(2,1)S(1)} %get-tuple-element.25), channel_id=1, source_target_pairs={{0,64},{4,68},{8,72},{12,76},{16,80},{20,84},{24,88},{28,92},{32,9... | collective-permute-start | bytes 1179656 | tf_op jit(solution)/shard_map/ppermute | solution.py:417
  11.1 2.5 %collective-permute-start.1 = (bf16[256,2,384]{2,1,0:T(2,128)(2,1)S(1)}, bf16[256,2,384]{2,1,0:T(2,128)(2,1)S(1)}, u32[]{:S(2)}, u32[]{:S(2)}) collective-permute-start(bf16[256,2,384]{2,1,0:T(2,128)(2,1)S(1)} %get-tuple-element.26), channel_id=1, source_target_pairs={{0,128},{4,132},{8,136},{12,140},{16,144},{20,148},{24,152},{28,15... | collective-permute-start | bytes 1179656 | tf_op jit(solution)/shard_map/ppermute | solution.py:417
  13.5 1.2 %collective-permute-start.2 = (bf16[256,2,384]{2,1,0:T(2,128)(2,1)S(1)}, bf16[256,2,384]{2,1,0:T(2,128)(2,1)}, u32[]{:S(2)}, u32[]{:S(2)}) collective-permute-start(bf16[256,2,384]{2,1,0:T(2,128)(2,1)S(1)} %get-tuple-element.27), channel_id=1, source_target_pairs={{0,192},{4,196},{8,200},{12,204},{16,208},{20,212},{24,216},{28,22... | collective-permute-start | bytes 1179656 | tf_op jit(solution)/shard_map/ppermute | solution.py:417
  14.7 16.2 %project.1 = (bf16[4,336,384]{2,1,0:T(8,128)(2,1)}, bf16[4,256,384]{2,1,0:T(8,128)(2,1)}, bf16[4,256,384]{2,1,0:T(8,128)(2,1)}) custom-call(s32[7]{0:T(128)} %stack.40.s_ref, bf16[256,4,2432]{2,1,0:T(4,128)(2,1)} %bitcast.27, bf16[16,3,4,2432]{3,2,1,0:T(4,128)(2,1)} %bitcast.31, f32[2,64]{1,0:T(2,128)} %gain_ref.1, bf16[3,2432,384]{2,1,0:T(8,128)(2,1)} %bitcast.29, ...), custom_call_target="tpu_custom_call" | custom-call | flops 1000 | bytes 1000 | tf_op jit(solution)/shard_map/project/pallas_call | solution.py:158
  30.9 0.0 collective-permute-done.refs_2_
  31.0 0.0 collective-permute-done.1.refs_3_
  31.0 0.0 collective-permute-done.2.refs_4_
  31.0 4.5 %all-to-all-start = ((bf16[4,336,384]{2,1,0:T(8,128)(2,1)}), bf16[4,336,384]{2,1,0:T(8,128)(2,1)}, u32[]{:S(2)}, u32[]{:S(2)}) async-start(bf16[4,336,384]{2,1,0:T(8,128)(2,1)} %get-tuple-element.28.q_ref), calls=%async_computation | async-start | bytes 2064384 | tf_op jit(solution)/shard_map/all_to_all | solution.py:427
  35.5 4.6 %own.1 = (bf16[4,72,384]{2,1,0:T(8,128)(2,1)}, bf16[4,72,384]{2,1,0:T(8,128)(2,1)}, bf16[4,72,384]{2,1,0:T(8,128)(2,1)}, bf16[4,72,384]{2,1,0:T(8,128)(2,1)}) custom-call(s32[7]{0:T(128)} %stack.40.s_ref, bf16[4,336,384]{2,1,0:T(8,128)(2,1)} %get-tuple-element.28.q_ref, bf16[4,256,384]{2,1,0:T(8,128)(2,1)} %get-tuple-element.32.k_ref, ...), custom_call_target="tpu_custom_call" | custom-call | flops 1000 | bytes 1000 | tf_op jit(solution)/shard_map/own/pallas_call | solution.py:228
  40.2 0.1 collective-permute-start.3
  40.3 0.1 collective-permute-start.4
  40.4 2.0 %collective-permute-start.5 = (bf16[4,72,384]{2,1,0:T(8,128)(2,1)}, bf16[4,72,384]{2,1,0:T(8,128)(2,1)S(1)}, u32[]{:S(2)}, u32[]{:S(2)}) collective-permute-start(bf16[4,72,384]{2,1,0:T(8,128)(2,1)} %get-tuple-element.37), channel_id=1, source_target_pairs={{0,3},{1,2},{2,1},{3,0},{4,7},{5,6},{6,5},{7,4},{8,11},{9,10},{10,... | collective-permute-start | bytes 663560 | tf_op jit(solution)/shard_map/ppermute | solution.py:431
  42.4 0.0 collective-permute-start.6
  42.4 0.0 collective-permute-done.7.w2
  42.4 0.5 collective-permute-start.8
  42.9 6.2 %all-to-all-done.refs_0_ = bf16[4,336,384]{2,1,0:T(8,128)(2,1)} async-done(((bf16[4,336,384]{2,1,0:T(8,128)(2,1)}), bf16[4,336,384]{2,1,0:T(8,128)(2,1)}, u32[]{:S(2)}, u32[]{:S(2)}) %all-to-all-start) | async-done | bytes 1032224 | tf_op jit(solution)/shard_map/all_to_all | solution.py:427
  49.1 11.4 %remote.1 = bf16[16,72,384]{2,1,0:T(8,128)(2,1)} custom-call(s32[7]{0:T(128)} %stack.40.s_ref, s32[4,16]{1,0:T(4,128)} %bitcast.38, bf16[4,336,384]{2,1,0:T(8,128)(2,1)} %all-to-all-done.refs_0_, bf16[256,4,2,384]{3,2,1,0:T(2,128)(2,1)} %bitcast.30, bf16[256,2,384]{2,1,0:T(2,128)(2,1)} %copy-done.3, bf16[256,2,384]{2,1,0:T(2,128)(2,1)} %copy-done.4, ...), custom_call_target="tpu_custom_call" | custom-call | flops 1000 | bytes 1000 | tf_op jit(solution)/shard_map/remote/pallas_call | solution.py:301
  60.5 0.0 collective-permute-done.3.near1
  60.5 0.0 copy-start.5
  60.6 0.0 collective-permute-done.4.near2
  60.6 0.0 collective-permute-done.5.near3
  60.6 3.9 %all-to-all-start.1 = ((bf16[16,72,384]{2,1,0:T(8,128)(2,1)}), bf16[16,72,384]{2,1,0:T(8,128)(2,1)S(1)}, u32[]{:S(2)}, u32[]{:S(2)}) async-start(bf16[16,72,384]{2,1,0:T(8,128)(2,1)} %remote.1), calls=%async_computation.1 | async-start | bytes 1769472 | tf_op jit(solution)/shard_map/all_to_all | solution.py:435
  64.6 0.2 maximum_bitcast_fusion
  64.8 2.8 %copy.10 = bf16[1,256,4,2,384]{4,3,2,1,0:T(2,128)(2,1)} copy(bf16[1,256,4,2,384]{4,1,2,3,0:T(8,128)(2,1)S(1)} %maximum_bitcast_fusion) | data formatting | bytes 3145728
  67.5 0.0 collective-permute-done.6.w1
  67.5 9.9 %all-to-all-done.1 = bf16[16,72,384]{2,1,0:T(8,128)(2,1)S(1)} async-done(((bf16[16,72,384]{2,1,0:T(8,128)(2,1)}), bf16[16,72,384]{2,1,0:T(8,128)(2,1)S(1)}, u32[]{:S(2)}, u32[]{:S(2)}) %all-to-all-start.1) | async-done | bytes 884768 | tf_op jit(solution)/shard_map/all_to_all | solution.py:435
  77.5 0.0 collective-permute-done.8.w3
  77.5 0.9 %copy-done = bf16[16,72,384]{2,1,0:T(8,128)(2,1)} copy-done((bf16[16,72,384]{2,1,0:T(8,128)(2,1)}, bf16[16,72,384]{2,1,0:T(8,128)(2,1)S(1)}, u32[]{:S(2)}) %copy-start) | copy-done | bytes 884760
  78.4 9.7 %finish.1 = bf16[64,4,2432]{2,1,0:T(4,128)(2,1)} custom-call(s32[7]{0:T(128)} %stack.40.s_ref, bf16[4,4,72,384]{3,2,1,0:T(8,128)(2,1)} %bitcast.33, bf16[4,72,384]{2,1,0:T(8,128)(2,1)} %get-tuple-element.39.near0, bf16[4,72,384]{2,1,0:T(8,128)(2,1)} %copy-done.5, bf16[4,72,384]{2,1,0:T(8,128)(2,1)} %copy-done.6, bf16[4,72,384]{2,1,0:T(8,128)(2,1)} %copy-done.7, ...), custom_call_target="tpu_custom_call" | custom-call | flops 1000 | bytes 1000 | tf_op jit(solution)/shard_map/finish/pallas_call | solution.py:393
  (14 shorter events, 0.0 us)
Async XLA Ops:
  3.5 38.9 %collective-permute-start.7 = (bf16[384,2432]{1,0:T(8,128)(2,1)}, bf16[384,2432]{1,0:T(8,128)(2,1)}, u32[]{:S(2)}, u32[]{:S(2)}) collective-permute-start(bf16[384,2432]{1,0:T(8,128)(2,1)} %w_own.1), channel_id=1, source_target_pairs={{0,2},{1,15},{2,0},{3,5},{4,6},{5,3},{6,4},{7,9},{8,10},{9,7},{10,... | collective-permute-start | bytes 5603336 | tf_op jit(solution)/shard_map/ppermute | solution.py:422
  9.9 21.1 %collective-permute-start = (bf16[256,2,384]{2,1,0:T(2,128)(2,1)S(1)}, bf16[256,2,384]{2,1,0:T(2,128)(2,1)S(1)}, u32[]{:S(2)}, u32[]{:S(2)}) collective-permute-start(bf16[256,2,384]{2,1,0:T(2,128)(2,1)S(1)} %get-tuple-element.25), channel_id=1, source_target_pairs={{0,64},{4,68},{8,72},{12,76},{16,80},{20,84},{24,88},{28,92},{32,9... | collective-permute-start | bytes 1179656 | tf_op jit(solution)/shard_map/ppermute | solution.py:417
  11.1 19.9 %collective-permute-start.1 = (bf16[256,2,384]{2,1,0:T(2,128)(2,1)S(1)}, bf16[256,2,384]{2,1,0:T(2,128)(2,1)S(1)}, u32[]{:S(2)}, u32[]{:S(2)}) collective-permute-start(bf16[256,2,384]{2,1,0:T(2,128)(2,1)S(1)} %get-tuple-element.26), channel_id=1, source_target_pairs={{0,128},{4,132},{8,136},{12,140},{16,144},{20,148},{24,152},{28,15... | collective-permute-start | bytes 1179656 | tf_op jit(solution)/shard_map/ppermute | solution.py:417
  13.5 17.4 %collective-permute-start.2 = (bf16[256,2,384]{2,1,0:T(2,128)(2,1)S(1)}, bf16[256,2,384]{2,1,0:T(2,128)(2,1)}, u32[]{:S(2)}, u32[]{:S(2)}) collective-permute-start(bf16[256,2,384]{2,1,0:T(2,128)(2,1)S(1)} %get-tuple-element.27), channel_id=1, source_target_pairs={{0,192},{4,196},{8,200},{12,204},{16,208},{20,212},{24,216},{28,22... | collective-permute-start | bytes 1179656 | tf_op jit(solution)/shard_map/ppermute | solution.py:417
  31.0 9.2 %copy-start.3 = (bf16[256,2,384]{2,1,0:T(2,128)(2,1)}, bf16[256,2,384]{2,1,0:T(2,128)(2,1)S(1)}, u32[]{:S(2)}) copy-start(bf16[256,2,384]{2,1,0:T(2,128)(2,1)S(1)} %collective-permute-done.refs_2_) | copy-start | bytes 1179652
  31.0 9.2 %copy-start.4 = (bf16[256,2,384]{2,1,0:T(2,128)(2,1)}, bf16[256,2,384]{2,1,0:T(2,128)(2,1)S(1)}, u32[]{:S(2)}) copy-start(bf16[256,2,384]{2,1,0:T(2,128)(2,1)S(1)} %collective-permute-done.1.refs_3_) | copy-start | bytes 1179652
  31.0 18.1 %all-to-all-start = ((bf16[4,336,384]{2,1,0:T(8,128)(2,1)}), bf16[4,336,384]{2,1,0:T(8,128)(2,1)}, u32[]{:S(2)}, u32[]{:S(2)}) async-start(bf16[4,336,384]{2,1,0:T(8,128)(2,1)} %get-tuple-element.28.q_ref), calls=%async_computation | async-start | bytes 2064384 | tf_op jit(solution)/shard_map/all_to_all | solution.py:427
  40.2 20.4 %collective-permute-start.3 = (bf16[4,72,384]{2,1,0:T(8,128)(2,1)}, bf16[4,72,384]{2,1,0:T(8,128)(2,1)S(1)}, u32[]{:S(2)}, u32[]{:S(2)}) collective-permute-start(bf16[4,72,384]{2,1,0:T(8,128)(2,1)} %get-tuple-element.35), channel_id=1, source_target_pairs={{0,1},{1,0},{2,3},{3,2},{4,5},{5,4},{6,7},{7,6},{8,9},{9,8},{10,11... | collective-permute-start | bytes 663560 | tf_op jit(solution)/shard_map/ppermute | solution.py:431
  40.3 20.3 %collective-permute-start.4 = (bf16[4,72,384]{2,1,0:T(8,128)(2,1)}, bf16[4,72,384]{2,1,0:T(8,128)(2,1)S(1)}, u32[]{:S(2)}, u32[]{:S(2)}) collective-permute-start(bf16[4,72,384]{2,1,0:T(8,128)(2,1)} %get-tuple-element.36), channel_id=1, source_target_pairs={{0,2},{1,3},{2,0},{3,1},{4,6},{5,7},{6,4},{7,5},{8,10},{9,11},{10,... | collective-permute-start | bytes 663560 | tf_op jit(solution)/shard_map/ppermute | solution.py:431
  40.4 20.2 %collective-permute-start.5 = (bf16[4,72,384]{2,1,0:T(8,128)(2,1)}, bf16[4,72,384]{2,1,0:T(8,128)(2,1)S(1)}, u32[]{:S(2)}, u32[]{:S(2)}) collective-permute-start(bf16[4,72,384]{2,1,0:T(8,128)(2,1)} %get-tuple-element.37), channel_id=1, source_target_pairs={{0,3},{1,2},{2,1},{3,0},{4,7},{5,6},{6,5},{7,4},{8,11},{9,10},{10,... | collective-permute-start | bytes 663560 | tf_op jit(solution)/shard_map/ppermute | solution.py:431
  42.4 25.1 %collective-permute-start.6 = (bf16[384,2432]{1,0:T(8,128)(2,1)}, bf16[384,2432]{1,0:T(8,128)(2,1)}, u32[]{:S(2)}, u32[]{:S(2)}) collective-permute-start(bf16[384,2432]{1,0:T(8,128)(2,1)} %w_own.1), channel_id=1, source_target_pairs={{0,1},{1,0},{2,3},{3,2},{4,5},{5,4},{6,7},{7,6},{8,9},{9,8},{10,11... | collective-permute-start | bytes 5603336 | tf_op jit(solution)/shard_map/ppermute | solution.py:423
  42.4 35.1 %collective-permute-start.8 = (bf16[384,2432]{1,0:T(8,128)(2,1)}, bf16[384,2432]{1,0:T(8,128)(2,1)}, u32[]{:S(2)}, u32[]{:S(2)}) collective-permute-start(bf16[384,2432]{1,0:T(8,128)(2,1)} %collective-permute-done.7.w2), channel_id=1, source_target_pairs={{0,1},{1,0},{2,3},{3,2},{4,5},{5,4},{6,7},{7,6},{8,9},{9,8},{10,11... | collective-permute-start | bytes 5603336 | tf_op jit(solution)/shard_map/ppermute | solution.py:428
  60.5 4.0 %copy-start.1 = (bf16[4,256,384]{2,1,0:T(8,128)(2,1)S(1)}, bf16[4,256,384]{2,1,0:T(8,128)(2,1)}, u32[]{:S(2)}) copy-start(bf16[4,256,384]{2,1,0:T(8,128)(2,1)} %get-tuple-element.32.k_ref) | copy-start | bytes 2359300
  60.5 4.0 %copy-start.2 = (bf16[4,256,384]{2,1,0:T(8,128)(2,1)S(1)}, bf16[4,256,384]{2,1,0:T(8,128)(2,1)}, u32[]{:S(2)}) copy-start(bf16[4,256,384]{2,1,0:T(8,128)(2,1)} %get-tuple-element.33.v_ref) | copy-start | bytes 2359300
  60.5 4.2 %copy-start.5 = (bf16[4,72,384]{2,1,0:T(8,128)(2,1)}, bf16[4,72,384]{2,1,0:T(8,128)(2,1)S(1)}, u32[]{:S(2)}) copy-start(bf16[4,72,384]{2,1,0:T(8,128)(2,1)S(1)} %collective-permute-done.3.near1) | copy-start | bytes 663556
  60.6 4.2 %copy-start.6 = (bf16[4,72,384]{2,1,0:T(8,128)(2,1)}, bf16[4,72,384]{2,1,0:T(8,128)(2,1)S(1)}, u32[]{:S(2)}) copy-start(bf16[4,72,384]{2,1,0:T(8,128)(2,1)S(1)} %collective-permute-done.4.near2) | copy-start | bytes 663556
  60.6 4.2 %copy-start.7 = (bf16[4,72,384]{2,1,0:T(8,128)(2,1)}, bf16[4,72,384]{2,1,0:T(8,128)(2,1)S(1)}, u32[]{:S(2)}) copy-start(bf16[4,72,384]{2,1,0:T(8,128)(2,1)S(1)} %collective-permute-done.5.near3) | copy-start | bytes 663556
  60.6 16.9 %all-to-all-start.1 = ((bf16[16,72,384]{2,1,0:T(8,128)(2,1)}), bf16[16,72,384]{2,1,0:T(8,128)(2,1)S(1)}, u32[]{:S(2)}, u32[]{:S(2)}) async-start(bf16[16,72,384]{2,1,0:T(8,128)(2,1)} %remote.1), calls=%async_computation.1 | async-start | bytes 1769472 | tf_op jit(solution)/shard_map/all_to_all | solution.py:435
  77.5 0.9 %copy-start = (bf16[16,72,384]{2,1,0:T(8,128)(2,1)}, bf16[16,72,384]{2,1,0:T(8,128)(2,1)S(1)}, u32[]{:S(2)}) copy-start(bf16[16,72,384]{2,1,0:T(8,128)(2,1)S(1)} %all-to-all-done.1) | copy-start | bytes 2654212

commit v4 on v3

--- a/solution.py
+++ b/solution.py
@@ -394,7 +394,7 @@
         finish_kernel,
         grid_spec=grid_spec,
         out_shape=jax.ShapeDtypeStruct((share, items, width_d), BF),
-        compiler_params=params(60),
+        compiler_params=params(54),
         cost_estimate=COST,
         name="finish",
     )(scalars, far, *near, hidden, modulation, *ws)

time: 88.8 us -> 88.8 us (level)
  no operation moved by 1% of the time
where the time goes in v4:
time: 88.8 us; the launch traced here: 88.3 us
  Pallas kernels  42 us (47%)
  starting transfers between devices  22.4 us (25%)
  waiting for transfers between devices  16.1 us (18%)
  local copies, waits for them, and re-layouts  6.45 us (7%)
  between operations  1.15 us (1%)
    pallas_call x1, Pallas kernels, project(): pl.pallas_call(project_kernel, grid_spec=grid_spec, out_shape=[jax.ShapeD...  16.2 us
    pallas_call x1, Pallas kernels, remote_attention(): pl.pallas_call(remote_kernel, grid_spec=grid_spec, out_shape=jax.ShapeDty...  11.4 us
    all_to_all x1, waiting for transfers between devices, body(): far = lax.all_to_all(sent, both, 0, 0, axis_index_groups=rings, tiled=True)  9.93 us
    pallas_call x1, Pallas kernels, finish(): pl.pallas_call(finish_kernel, grid_spec=grid_spec, out_shape=jax.ShapeDty...  9.72 us
    ppermute x1, starting transfers between devices, body(): w_far = lax.ppermute(w_own, both, w_pairs)  6.41 us
    all_to_all x1, waiting for transfers between devices, body(): lax.all_to_all(q_sent, 'req', 0, 0, axis_index_groups=columns, tiled=True)  6.18 us
    ppermute x3, starting transfers between devices, along_x(): lax.ppermute(value, 'req', [(i, (i + by * groups) % slots) for i in range...  4.82 us
    pallas_call x1, Pallas kernels, own_attention(): pl.pallas_call(own_kernel, in_specs=[pl.BlockSpec(memory_space=pltpu.SMEM...  4.63 us
  transfers between devices with their start and end apart: 11, of which 2 were waited for; matrix products, arithmetic and copies ran while one was open for 3% of the time, Pallas kernels for 37%

profile of v4, /device:TPU:1, one launch (start us, length us, event | category | flops | bytes accessed | tf_op | source)
XLA Modules:
  0.0 88.3 jit_solution(2214753919586270131)
XLA Ops:
  0.7 2.1 %dynamic-slice_bitcast_fusion = (bf16[256,2,384]{2,1,0:T(2,128)(2,1)S(1)}, bf16[256,2,384]{2,1,0:T(2,128)(2,1)S(1)}, bf16[256,2,384]{2,1,0:T(2,128)(2,1)S(1)}) fusion(bf16[1,256,4,2,384]{4,3,2,1,0:T(2,128)(2,1)} %param.13, s32[]{:T(128)S(6)} %select_n.43, s32[]{:T(128)S(6)} %select_n.41, s32[]{:T(128)S(6)} %select_n.39), kind=kLoop, calls=%fused_computation.1 | loop fusion | bytes 2359308 | tf_op jit(solution)/shard_map/jit(dynamic_index_in_dim)/squeeze | solution.py:419
  2.8 0.7 stack.40.s_ref
  3.5 6.4 %collective-permute-start.7 = (bf16[384,2432]{1,0:T(8,128)(2,1)}, bf16[384,2432]{1,0:T(8,128)(2,1)}, u32[]{:S(2)}, u32[]{:S(2)}) collective-permute-start(bf16[384,2432]{1,0:T(8,128)(2,1)} %w_own.1), channel_id=1, source_target_pairs={{0,2},{1,15},{2,0},{3,5},{4,6},{5,3},{6,4},{7,9},{8,10},{9,7},{10,... | collective-permute-start | bytes 5603336 | tf_op jit(solution)/shard_map/ppermute | solution.py:422
  9.9 1.2 %collective-permute-start = (bf16[256,2,384]{2,1,0:T(2,128)(2,1)S(1)}, bf16[256,2,384]{2,1,0:T(2,128)(2,1)S(1)}, u32[]{:S(2)}, u32[]{:S(2)}) collective-permute-start(bf16[256,2,384]{2,1,0:T(2,128)(2,1)S(1)} %get-tuple-element.25), channel_id=1, source_target_pairs={{0,64},{4,68},{8,72},{12,76},{16,80},{20,84},{24,88},{28,92},{32,9... | collective-permute-start | bytes 1179656 | tf_op jit(solution)/shard_map/ppermute | solution.py:417
  11.1 2.5 %collective-permute-start.1 = (bf16[256,2,384]{2,1,0:T(2,128)(2,1)S(1)}, bf16[256,2,384]{2,1,0:T(2,128)(2,1)S(1)}, u32[]{:S(2)}, u32[]{:S(2)}) collective-permute-start(bf16[256,2,384]{2,1,0:T(2,128)(2,1)S(1)} %get-tuple-element.26), channel_id=1, source_target_pairs={{0,128},{4,132},{8,136},{12,140},{16,144},{20,148},{24,152},{28,15... | collective-permute-start | bytes 1179656 | tf_op jit(solution)/shard_map/ppermute | solution.py:417
  13.5 1.2 %collective-permute-start.2 = (bf16[256,2,384]{2,1,0:T(2,128)(2,1)S(1)}, bf16[256,2,384]{2,1,0:T(2,128)(2,1)}, u32[]{:S(2)}, u32[]{:S(2)}) collective-permute-start(bf16[256,2,384]{2,1,0:T(2,128)(2,1)S(1)} %get-tuple-element.27), channel_id=1, source_target_pairs={{0,192},{4,196},{8,200},{12,204},{16,208},{20,212},{24,216},{28,22... | collective-permute-start | bytes 1179656 | tf_op jit(solution)/shard_map/ppermute | solution.py:417
  14.7 16.2 %project.1 = (bf16[4,336,384]{2,1,0:T(8,128)(2,1)}, bf16[4,256,384]{2,1,0:T(8,128)(2,1)}, bf16[4,256,384]{2,1,0:T(8,128)(2,1)}) custom-call(s32[7]{0:T(128)} %stack.40.s_ref, bf16[256,4,2432]{2,1,0:T(4,128)(2,1)} %bitcast.27, bf16[16,3,4,2432]{3,2,1,0:T(4,128)(2,1)} %bitcast.31, f32[2,64]{1,0:T(2,128)} %gain_ref.1, bf16[3,2432,384]{2,1,0:T(8,128)(2,1)} %bitcast.29, ...), custom_call_target="tpu_custom_call" | custom-call | flops 1000 | bytes 1000 | tf_op jit(solution)/shard_map/project/pallas_call | solution.py:158
  30.9 0.0 collective-permute-done.refs_2_
  31.0 0.0 collective-permute-done.1.refs_3_
  31.0 0.0 collective-permute-done.2.refs_4_
  31.0 4.5 %all-to-all-start = ((bf16[4,336,384]{2,1,0:T(8,128)(2,1)}), bf16[4,336,384]{2,1,0:T(8,128)(2,1)}, u32[]{:S(2)}, u32[]{:S(2)}) async-start(bf16[4,336,384]{2,1,0:T(8,128)(2,1)} %get-tuple-element.28.q_ref), calls=%async_computation | async-start | bytes 2064384 | tf_op jit(solution)/shard_map/all_to_all | solution.py:427
  35.5 4.6 %own.1 = (bf16[4,72,384]{2,1,0:T(8,128)(2,1)}, bf16[4,72,384]{2,1,0:T(8,128)(2,1)}, bf16[4,72,384]{2,1,0:T(8,128)(2,1)}, bf16[4,72,384]{2,1,0:T(8,128)(2,1)}) custom-call(s32[7]{0:T(128)} %stack.40.s_ref, bf16[4,336,384]{2,1,0:T(8,128)(2,1)} %get-tuple-element.28.q_ref, bf16[4,256,384]{2,1,0:T(8,128)(2,1)} %get-tuple-element.32.k_ref, ...), custom_call_target="tpu_custom_call" | custom-call | flops 1000 | bytes 1000 | tf_op jit(solution)/shard_map/own/pallas_call | solution.py:228
  40.2 0.1 collective-permute-start.3
  40.3 0.1 collective-permute-start.4
  40.4 2.0 %collective-permute-start.5 = (bf16[4,72,384]{2,1,0:T(8,128)(2,1)}, bf16[4,72,384]{2,1,0:T(8,128)(2,1)S(1)}, u32[]{:S(2)}, u32[]{:S(2)}) collective-permute-start(bf16[4,72,384]{2,1,0:T(8,128)(2,1)} %get-tuple-element.37), channel_id=1, source_target_pairs={{0,3},{1,2},{2,1},{3,0},{4,7},{5,6},{6,5},{7,4},{8,11},{9,10},{10,... | collective-permute-start | bytes 663560 | tf_op jit(solution)/shard_map/ppermute | solution.py:431
  42.4 0.0 collective-permute-start.6
  42.4 0.0 collective-permute-done.7.w2
  42.4 0.5 collective-permute-start.8
  42.9 6.2 %all-to-all-done.refs_0_ = bf16[4,336,384]{2,1,0:T(8,128)(2,1)} async-done(((bf16[4,336,384]{2,1,0:T(8,128)(2,1)}), bf16[4,336,384]{2,1,0:T(8,128)(2,1)}, u32[]{:S(2)}, u32[]{:S(2)}) %all-to-all-start) | async-done | bytes 1032224 | tf_op jit(solution)/shard_map/all_to_all | solution.py:427
  49.1 11.4 %remote.1 = bf16[16,72,384]{2,1,0:T(8,128)(2,1)} custom-call(s32[7]{0:T(128)} %stack.40.s_ref, s32[4,16]{1,0:T(4,128)} %bitcast.38, bf16[4,336,384]{2,1,0:T(8,128)(2,1)} %all-to-all-done.refs_0_, bf16[256,4,2,384]{3,2,1,0:T(2,128)(2,1)} %bitcast.30, bf16[256,2,384]{2,1,0:T(2,128)(2,1)} %copy-done.3, bf16[256,2,384]{2,1,0:T(2,128)(2,1)} %copy-done.4, ...), custom_call_target="tpu_custom_call" | custom-call | flops 1000 | bytes 1000 | tf_op jit(solution)/shard_map/remote/pallas_call | solution.py:301
  60.5 0.0 collective-permute-done.3.near1
  60.5 0.0 copy-start.5
  60.6 0.0 collective-permute-done.4.near2
  60.6 0.0 collective-permute-done.5.near3
  60.6 3.9 %all-to-all-start.1 = ((bf16[16,72,384]{2,1,0:T(8,128)(2,1)}), bf16[16,72,384]{2,1,0:T(8,128)(2,1)S(1)}, u32[]{:S(2)}, u32[]{:S(2)}) async-start(bf16[16,72,384]{2,1,0:T(8,128)(2,1)} %remote.1), calls=%async_computation.1 | async-start | bytes 1769472 | tf_op jit(solution)/shard_map/all_to_all | solution.py:435
  64.6 0.2 maximum_bitcast_fusion
  64.8 2.8 %copy.10 = bf16[1,256,4,2,384]{4,3,2,1,0:T(2,128)(2,1)} copy(bf16[1,256,4,2,384]{4,1,2,3,0:T(8,128)(2,1)S(1)} %maximum_bitcast_fusion) | data formatting | bytes 3145728
  67.5 0.0 collective-permute-done.6.w1
  67.5 9.9 %all-to-all-done.1 = bf16[16,72,384]{2,1,0:T(8,128)(2,1)S(1)} async-done(((bf16[16,72,384]{2,1,0:T(8,128)(2,1)}), bf16[16,72,384]{2,1,0:T(8,128)(2,1)S(1)}, u32[]{:S(2)}, u32[]{:S(2)}) %all-to-all-start.1) | async-done | bytes 884768 | tf_op jit(solution)/shard_map/all_to_all | solution.py:435
  77.5 0.0 collective-permute-done.8.w3
  77.5 0.9 %copy-done = bf16[16,72,384]{2,1,0:T(8,128)(2,1)} copy-done((bf16[16,72,384]{2,1,0:T(8,128)(2,1)}, bf16[16,72,384]{2,1,0:T(8,128)(2,1)S(1)}, u32[]{:S(2)}) %copy-start) | copy-done | bytes 884760
  78.4 9.7 %finish.1 = bf16[64,4,2432]{2,1,0:T(4,128)(2,1)} custom-call(s32[7]{0:T(128)} %stack.40.s_ref, bf16[4,4,72,384]{3,2,1,0:T(8,128)(2,1)} %bitcast.33, bf16[4,72,384]{2,1,0:T(8,128)(2,1)} %get-tuple-element.39.near0, bf16[4,72,384]{2,1,0:T(8,128)(2,1)} %copy-done.5, bf16[4,72,384]{2,1,0:T(8,128)(2,1)} %copy-done.6, bf16[4,72,384]{2,1,0:T(8,128)(2,1)} %copy-done.7, ...), custom_call_target="tpu_custom_call" | custom-call | flops 1000 | bytes 1000 | tf_op jit(solution)/shard_map/finish/pallas_call | solution.py:393
  (14 shorter events, 0.0 us)
Async XLA Ops:
  3.5 38.9 %collective-permute-start.7 = (bf16[384,2432]{1,0:T(8,128)(2,1)}, bf16[384,2432]{1,0:T(8,128)(2,1)}, u32[]{:S(2)}, u32[]{:S(2)}) collective-permute-start(bf16[384,2432]{1,0:T(8,128)(2,1)} %w_own.1), channel_id=1, source_target_pairs={{0,2},{1,15},{2,0},{3,5},{4,6},{5,3},{6,4},{7,9},{8,10},{9,7},{10,... | collective-permute-start | bytes 5603336 | tf_op jit(solution)/shard_map/ppermute | solution.py:422
  9.9 21.1 %collective-permute-start = (bf16[256,2,384]{2,1,0:T(2,128)(2,1)S(1)}, bf16[256,2,384]{2,1,0:T(2,128)(2,1)S(1)}, u32[]{:S(2)}, u32[]{:S(2)}) collective-permute-start(bf16[256,2,384]{2,1,0:T(2,128)(2,1)S(1)} %get-tuple-element.25), channel_id=1, source_target_pairs={{0,64},{4,68},{8,72},{12,76},{16,80},{20,84},{24,88},{28,92},{32,9... | collective-permute-start | bytes 1179656 | tf_op jit(solution)/shard_map/ppermute | solution.py:417
  11.1 19.9 %collective-permute-start.1 = (bf16[256,2,384]{2,1,0:T(2,128)(2,1)S(1)}, bf16[256,2,384]{2,1,0:T(2,128)(2,1)S(1)}, u32[]{:S(2)}, u32[]{:S(2)}) collective-permute-start(bf16[256,2,384]{2,1,0:T(2,128)(2,1)S(1)} %get-tuple-element.26), channel_id=1, source_target_pairs={{0,128},{4,132},{8,136},{12,140},{16,144},{20,148},{24,152},{28,15... | collective-permute-start | bytes 1179656 | tf_op jit(solution)/shard_map/ppermute | solution.py:417
  13.5 17.4 %collective-permute-start.2 = (bf16[256,2,384]{2,1,0:T(2,128)(2,1)S(1)}, bf16[256,2,384]{2,1,0:T(2,128)(2,1)}, u32[]{:S(2)}, u32[]{:S(2)}) collective-permute-start(bf16[256,2,384]{2,1,0:T(2,128)(2,1)S(1)} %get-tuple-element.27), channel_id=1, source_target_pairs={{0,192},{4,196},{8,200},{12,204},{16,208},{20,212},{24,216},{28,22... | collective-permute-start | bytes 1179656 | tf_op jit(solution)/shard_map/ppermute | solution.py:417
  31.0 9.2 %copy-start.3 = (bf16[256,2,384]{2,1,0:T(2,128)(2,1)}, bf16[256,2,384]{2,1,0:T(2,128)(2,1)S(1)}, u32[]{:S(2)}) copy-start(bf16[256,2,384]{2,1,0:T(2,128)(2,1)S(1)} %collective-permute-done.refs_2_) | copy-start | bytes 1179652
  31.0 9.2 %copy-start.4 = (bf16[256,2,384]{2,1,0:T(2,128)(2,1)}, bf16[256,2,384]{2,1,0:T(2,128)(2,1)S(1)}, u32[]{:S(2)}) copy-start(bf16[256,2,384]{2,1,0:T(2,128)(2,1)S(1)} %collective-permute-done.1.refs_3_) | copy-start | bytes 1179652
  31.0 18.1 %all-to-all-start = ((bf16[4,336,384]{2,1,0:T(8,128)(2,1)}), bf16[4,336,384]{2,1,0:T(8,128)(2,1)}, u32[]{:S(2)}, u32[]{:S(2)}) async-start(bf16[4,336,384]{2,1,0:T(8,128)(2,1)} %get-tuple-element.28.q_ref), calls=%async_computation | async-start | bytes 2064384 | tf_op jit(solution)/shard_map/all_to_all | solution.py:427
  40.2 20.4 %collective-permute-start.3 = (bf16[4,72,384]{2,1,0:T(8,128)(2,1)}, bf16[4,72,384]{2,1,0:T(8,128)(2,1)S(1)}, u32[]{:S(2)}, u32[]{:S(2)}) collective-permute-start(bf16[4,72,384]{2,1,0:T(8,128)(2,1)} %get-tuple-element.35), channel_id=1, source_target_pairs={{0,1},{1,0},{2,3},{3,2},{4,5},{5,4},{6,7},{7,6},{8,9},{9,8},{10,11... | collective-permute-start | bytes 663560 | tf_op jit(solution)/shard_map/ppermute | solution.py:431
  40.3 20.3 %collective-permute-start.4 = (bf16[4,72,384]{2,1,0:T(8,128)(2,1)}, bf16[4,72,384]{2,1,0:T(8,128)(2,1)S(1)}, u32[]{:S(2)}, u32[]{:S(2)}) collective-permute-start(bf16[4,72,384]{2,1,0:T(8,128)(2,1)} %get-tuple-element.36), channel_id=1, source_target_pairs={{0,2},{1,3},{2,0},{3,1},{4,6},{5,7},{6,4},{7,5},{8,10},{9,11},{10,... | collective-permute-start | bytes 663560 | tf_op jit(solution)/shard_map/ppermute | solution.py:431
  40.4 20.2 %collective-permute-start.5 = (bf16[4,72,384]{2,1,0:T(8,128)(2,1)}, bf16[4,72,384]{2,1,0:T(8,128)(2,1)S(1)}, u32[]{:S(2)}, u32[]{:S(2)}) collective-permute-start(bf16[4,72,384]{2,1,0:T(8,128)(2,1)} %get-tuple-element.37), channel_id=1, source_target_pairs={{0,3},{1,2},{2,1},{3,0},{4,7},{5,6},{6,5},{7,4},{8,11},{9,10},{10,... | collective-permute-start | bytes 663560 | tf_op jit(solution)/shard_map/ppermute | solution.py:431
  42.4 25.1 %collective-permute-start.6 = (bf16[384,2432]{1,0:T(8,128)(2,1)}, bf16[384,2432]{1,0:T(8,128)(2,1)}, u32[]{:S(2)}, u32[]{:S(2)}) collective-permute-start(bf16[384,2432]{1,0:T(8,128)(2,1)} %w_own.1), channel_id=1, source_target_pairs={{0,1},{1,0},{2,3},{3,2},{4,5},{5,4},{6,7},{7,6},{8,9},{9,8},{10,11... | collective-permute-start | bytes 5603336 | tf_op jit(solution)/shard_map/ppermute | solution.py:423
  42.4 35.1 %collective-permute-start.8 = (bf16[384,2432]{1,0:T(8,128)(2,1)}, bf16[384,2432]{1,0:T(8,128)(2,1)}, u32[]{:S(2)}, u32[]{:S(2)}) collective-permute-start(bf16[384,2432]{1,0:T(8,128)(2,1)} %collective-permute-done.7.w2), channel_id=1, source_target_pairs={{0,1},{1,0},{2,3},{3,2},{4,5},{5,4},{6,7},{7,6},{8,9},{9,8},{10,11... | collective-permute-start | bytes 5603336 | tf_op jit(solution)/shard_map/ppermute | solution.py:428
  60.5 4.0 %copy-start.1 = (bf16[4,256,384]{2,1,0:T(8,128)(2,1)S(1)}, bf16[4,256,384]{2,1,0:T(8,128)(2,1)}, u32[]{:S(2)}) copy-start(bf16[4,256,384]{2,1,0:T(8,128)(2,1)} %get-tuple-element.32.k_ref) | copy-start | bytes 2359300
  60.5 4.0 %copy-start.2 = (bf16[4,256,384]{2,1,0:T(8,128)(2,1)S(1)}, bf16[4,256,384]{2,1,0:T(8,128)(2,1)}, u32[]{:S(2)}) copy-start(bf16[4,256,384]{2,1,0:T(8,128)(2,1)} %get-tuple-element.33.v_ref) | copy-start | bytes 2359300
  60.5 4.2 %copy-start.5 = (bf16[4,72,384]{2,1,0:T(8,128)(2,1)}, bf16[4,72,384]{2,1,0:T(8,128)(2,1)S(1)}, u32[]{:S(2)}) copy-start(bf16[4,72,384]{2,1,0:T(8,128)(2,1)S(1)} %collective-permute-done.3.near1) | copy-start | bytes 663556
  60.6 4.2 %copy-start.6 = (bf16[4,72,384]{2,1,0:T(8,128)(2,1)}, bf16[4,72,384]{2,1,0:T(8,128)(2,1)S(1)}, u32[]{:S(2)}) copy-start(bf16[4,72,384]{2,1,0:T(8,128)(2,1)S(1)} %collective-permute-done.4.near2) | copy-start | bytes 663556
  60.6 4.2 %copy-start.7 = (bf16[4,72,384]{2,1,0:T(8,128)(2,1)}, bf16[4,72,384]{2,1,0:T(8,128)(2,1)S(1)}, u32[]{:S(2)}) copy-start(bf16[4,72,384]{2,1,0:T(8,128)(2,1)S(1)} %collective-permute-done.5.near3) | copy-start | bytes 663556
  60.6 16.9 %all-to-all-start.1 = ((bf16[16,72,384]{2,1,0:T(8,128)(2,1)}), bf16[16,72,384]{2,1,0:T(8,128)(2,1)S(1)}, u32[]{:S(2)}, u32[]{:S(2)}) async-start(bf16[16,72,384]{2,1,0:T(8,128)(2,1)} %remote.1), calls=%async_computation.1 | async-start | bytes 1769472 | tf_op jit(solution)/shard_map/all_to_all | solution.py:435
  77.5 0.9 %copy-start = (bf16[16,72,384]{2,1,0:T(8,128)(2,1)}, bf16[16,72,384]{2,1,0:T(8,128)(2,1)S(1)}, u32[]{:S(2)}) copy-start(bf16[16,72,384]{2,1,0:T(8,128)(2,1)S(1)} %all-to-all-done.1) | copy-start | bytes 2654212
